TPU v7x, 512 devices: a whole 4x4x16 slice. The times are simulated.
512 devices in a mesh: section: 4 (over x), doc: 32 (over z, core), mp: 4 (over y).
Axes of the slice: x: 4, y: 4, z: 16, core: 2. Of those that a mesh axis runs over, the one named last changes fastest.
Arguments:
- queries: bfloat16 [64, 512, 8, 4, 128], P('doc', None, 'section', 'mp'), may hold values from -420 to 420
- cotangent: bfloat16 [64, 512, 8, 4, 128], P('doc', None, 'section', 'mp'), may hold values from -180 to 180
- cache: bfloat16 [512, 128, 4, 2, 128], P('doc', 'section', 'mp'), may hold values from -7 to 7
- momentum: float32 [512, 128, 4, 2, 128], P('doc', 'section', 'mp'), may hold values from -3 to 3
- doc_lists: int32 [64, 8], P('doc'), may hold values from 0 to 511, as said below
- place: int32 [512], replicated, may hold values from 0 to 511, as said below
Outputs:
- attention: bfloat16 [64, 512, 8, 4, 128], P('doc', None, 'section', 'mp')
- new_cache: bfloat16 [512, 128, 4, 2, 128], P('doc', 'section', 'mp')
- new_momentum: float32 [512, 128, 4, 2, 128], P('doc', 'section', 'mp')
Inputs may be any that keep to these rules, and one draw needn't show every extreme that they name: `doc_lists`: the 2 rows of one index of doc (an aligned block of rows) name 16 different documents in all. Counting each document's owner as place[document] // 16, those documents lie on at most 1 per owner. `place`: each row of cache holds exactly one document.
All inputs are finite; a program needn't handle non-finite values.
Results may differ from a plain program's by a relative error of at most 0.017.
Values may be sent and summed in bfloat16 or wider, within the bound.
No kernel may reach another device: no remote copies, remote signals or barrier semaphores. Data moves between devices by JAX's collectives and lax.ppermute only.
A program may use at most 64 MiB of HBM per device.

v0:
```python
import math

import jax
import jax.numpy as jnp
from jax import lax
from jax.sharding import PartitionSpec as P

momentum_decay = 0.9
step_rate = 0.3
clip_level = 0.5


def body(queries, cotangent, cache, momentum, doc_lists, place):
    rows_dev, seq_len, head_count, kv_count, head_size = queries.shape
    doc_dev, len_part = (cache.shape[0], cache.shape[1])
    doc_total = place.shape[0]
    owners = doc_total // doc_dev
    sections = lax.axis_size("section")
    list_len = doc_lists.shape[1]
    requests = rows_dev * list_len
    owner_used = min(owners, requests)
    capacity = (requests + owner_used - 1) // owner_used
    flat_width = kv_count * 2 * head_size
    score_scale = 1.0 / math.sqrt(head_size)
    everyone = lax.all_gather(doc_lists, "doc", axis=0, tiled=True).reshape(owners, requests)
    matches = (
        everyone[:, :, None] == jnp.arange(doc_total, dtype=jnp.int32)[None, None, :]
    ).astype(jnp.int32)
    positions = jnp.sum(matches * place[None, None, :], axis=-1)
    holder = positions // doc_dev
    local_slot = positions % doc_dev
    earlier = jnp.arange(requests)[:, None] > jnp.arange(requests)[None, :]
    same_owner = holder[:, :, None] == holder[:, None, :]
    slot_rank = jnp.sum((same_owner & earlier[None]).astype(jnp.int32), axis=-1)
    my_index = lax.axis_index("doc")
    my_holder = lax.dynamic_index_in_dim(holder, my_index, 0, keepdims=False)
    my_rank = lax.dynamic_index_in_dim(slot_rank, my_index, 0, keepdims=False)
    target = my_holder * capacity + my_rank
    claimed = (holder == my_index)[:, :, None] & (
        slot_rank[:, :, None] == jnp.arange(capacity)[None, None, :]
    )
    slot_table = jnp.sum(jnp.where(claimed, local_slot[:, :, None], 0), axis=1)
    filled = jnp.any(claimed, axis=1)
    stored = cache.reshape(doc_dev, len_part, flat_width)
    outgoing = jnp.where(filled[:, :, None, None], stored[slot_table], jnp.zeros((), jnp.bfloat16))
    fanned = jnp.broadcast_to(outgoing[None], (sections,) + outgoing.shape)
    fanned = fanned.reshape(sections * owners, capacity, len_part, flat_width)
    arrived = lax.all_to_all(fanned, ("section", "doc"), split_axis=0, concat_axis=0, tiled=True)
    arrived = arrived.reshape(sections, owners * capacity, len_part, flat_width)
    picked = arrived[:, target]
    fetched = jnp.moveaxis(picked, 0, 1).reshape(requests, sections * len_part, flat_width)
    length = fetched.shape[1]
    memory = fetched.reshape(rows_dev, list_len * length, kv_count, 2, head_size)

    def row_attention(operands):
        query_row, tangent_row, memory_row = operands
        query = query_row[:, :, 0, :].reshape(seq_len * head_count, head_size)
        tangent = tangent_row[:, :, 0, :].reshape(seq_len * head_count, head_size)
        key_rows = memory_row[:, 0, 0, :]
        value_rows = memory_row[:, 0, 1, :]
        scores = (
            jnp.einsum("qd,kd->qk", query, key_rows, preferred_element_type=jnp.float32)
            * score_scale
        )
        weights = jax.nn.softmax(scores, axis=-1)
        weight_bf = weights.astype(jnp.bfloat16)
        attended = jnp.dot(weight_bf, value_rows, preferred_element_type=jnp.float32).astype(
            jnp.bfloat16
        )
        row_delta = jnp.sum(
            attended.astype(jnp.float32) * tangent.astype(jnp.float32), axis=-1, keepdims=True
        )
        grad_weights = jnp.einsum(
            "qd,kd->qk", tangent, value_rows, preferred_element_type=jnp.float32
        )
        grad_scores = (weights * (grad_weights - row_delta) * score_scale).astype(jnp.bfloat16)
        grad_keys = jnp.einsum("qk,qd->kd", grad_scores, query, preferred_element_type=jnp.float32)
        grad_values = jnp.einsum(
            "qk,qd->kd", weight_bf, tangent, preferred_element_type=jnp.float32
        )
        grad_list = [jnp.stack([grad_keys, grad_values], axis=1).astype(jnp.bfloat16)]
        attended_list = [attended.reshape(seq_len, head_count, head_size)]
        return (jnp.stack(attended_list, axis=2), jnp.stack(grad_list, axis=1))

    attention, partial_value = lax.map(row_attention, (queries, cotangent, memory))
    partial_value = partial_value.reshape(requests, length, flat_width)
    pieces = partial_value.reshape(requests, sections, len_part, flat_width)
    parcel = (
        jnp.zeros((owners * capacity, sections, len_part, flat_width), jnp.bfloat16)
        .at[target]
        .set(pieces)
    )
    parcel = jnp.moveaxis(parcel, 1, 0).reshape(sections * owners, capacity, len_part, flat_width)
    returned = lax.all_to_all(parcel, ("section", "doc"), split_axis=0, concat_axis=0, tiled=True)
    returned = returned.reshape(sections, owners * capacity, len_part * flat_width).astype(
        jnp.float32
    )
    collected = jnp.sum(returned, axis=0)
    assign = (slot_table.reshape(-1)[None, :] == jnp.arange(doc_dev)[:, None]) & filled.reshape(-1)[
        None, :
    ]
    gradient = jnp.dot(
        assign.astype(jnp.float32),
        collected,
        precision=lax.Precision.HIGHEST,
        preferred_element_type=jnp.float32,
    )
    gradient = gradient.reshape(momentum.shape)
    norm_square = lax.psum(jnp.sum(gradient * gradient), ("section", "doc", "mp"))
    entry_count = doc_total * len_part * sections * kv_count * lax.axis_size("mp") * 2 * head_size
    clip_limit = clip_level * math.sqrt(entry_count)
    norm_value = jnp.sqrt(norm_square)
    factor = clip_limit / jnp.maximum(norm_value, clip_limit)
    new_momentum = momentum_decay * momentum + factor * gradient
    new_cache = (cache.astype(jnp.float32) - step_rate * new_momentum).astype(jnp.bfloat16)
    return (attention, new_cache, new_momentum)


def solution(mesh):
    in_specs = (
        P("doc", None, "section", "mp", None),
        P("doc", None, "section", "mp", None),
        P("doc", "section", "mp", None, None),
        P("doc", "section", "mp", None, None),
        P("doc", None),
        P(),
    )
    out_specs = (
        P("doc", None, "section", "mp", None),
        P("doc", "section", "mp", None, None),
        P("doc", "section", "mp", None, None),
    )
    return jax.shard_map(body, mesh=mesh, in_specs=in_specs, out_specs=out_specs, check_vma=False)
```

profile of v0, /device:TPU:1, one launch (start us, length us, event | category | flops | bytes accessed | tf_op | source)
XLA Modules:
  0.0 404.3 jit_solution(12242166268992438319)
XLA Ops:
  0.6 37.9 %all-gather = s32[32,2,8]{2,1,0:T(2,128)S(1)} all-gather(s32[1,2,8]{2,1,0:T(2,128)} %bitcast.94), channel_id=1, replica_groups=mesh['section'=4,'doc'=32,'mp'=4] {'doc'}, dimensions={0}, use_global_device_ids=true | all-gather | bytes 2112 | tf_op jit(solution)/shard_map/all_gather | solution.py:25
  38.7 1.4 select_reduce_fusion
  40.7 1.1 reshape.202
  42.5 1.6 broadcast_in_dim.32
  44.1 10.6 %all-to-all-start = ((bf16[128,1,32,256]{3,2,1,0:T(8,128)(2,1)}), bf16[128,1,32,256]{3,2,1,0:T(8,128)(2,1)S(1)}, u32[]{:S(2)}, u32[]{:S(2)}) async-start(bf16[128,1,32,256]{3,2,1,0:T(8,128)(2,1)} %bitcast.12), calls=%async_computation | async-start | bytes 4194304 | tf_op jit(solution)/shard_map/all_to_all | solution.py:48
  54.8 99.1 %all-to-all-done = bf16[128,1,32,256]{3,2,1,0:T(8,128)(2,1)S(1)} async-done(((bf16[128,1,32,256]{3,2,1,0:T(8,128)(2,1)}), bf16[128,1,32,256]{3,2,1,0:T(8,128)(2,1)S(1)}, u32[]{:S(2)}, u32[]{:S(2)}) %all-to-all-start) | async-done | bytes 2097184 | tf_op jit(solution)/shard_map/all_to_all | solution.py:48
  154.8 28.1 %while.12 = (s32[]{:T(128)}, bf16[2,512,2,1,128]{4,2,1,3,0:T(2,128)(2,1)}, bf16[2,1024,1,2,128]{4,3,1,0,2:T(2,128)(2,1)}, bf16[2,512,2,1,128]{4,2,3,1,0:T(2,128)...) while((s32[]{:T(128)}, ...), condition=%wide.region_8.9_spmd, body=%wide.region_4.8_spmd.sunk | while | flops 1364325376 | bytes 61124872 | solution.py:85
  155.3 1.1 constant_dynamic-slice_fusion.8
  158.1 1.3 multiply_reduce_fusion.6
  159.4 3.6 fusion.45
  163.0 3.2 fusion.44
  166.9 1.0 copy-done.3
  169.4 1.1 constant_dynamic-slice_fusion.8
  172.2 1.3 multiply_reduce_fusion.6
  173.4 3.6 fusion.45
  177.1 3.2 fusion.44
  183.0 1.7 reshape.226
  185.0 1.1 scatter_fusion
  186.3 107.8 %all_to_all.10 = bf16[128,1,32,256]{3,2,1,0:T(8,128)(2,1)S(1)} all-to-all(bf16[128,1,32,256]{3,2,1,0:T(8,128)(2,1)S(1)} %bitcast.86), channel_id=1, replica_groups=mesh['section'=4,'doc'=32,'mp'=4] {'section','doc'}, dimensions={0} | all-to-all | bytes 4194304 | tf_op jit(solution)/shard_map/all_to_all | solution.py:94
  294.1 2.8 reshape.205
  296.8 2.6 reduce_sum.69
  299.4 1.2 multiply_reduce_fusion.2
  300.6 100.9 %psum.7 = f32[]{:T(128)} all-reduce(f32[]{:T(128)} %get-tuple-element.103), channel_id=1, replica_groups=mesh['section'=4,'doc'=32,'mp'=4] {'section','doc','mp'}, use_global_device_ids=true, to_apply=%region_12.13 | all-reduce | flops 1 | bytes 8 | tf_op jit(solution)/shard_map/psum | solution.py:109
  402.8 1.5 subtract_convert_fusion
  (66 shorter events, 11.6 us)
Async XLA Ops:
  44.1 109.8 %all-to-all-start = ((bf16[128,1,32,256]{3,2,1,0:T(8,128)(2,1)}), bf16[128,1,32,256]{3,2,1,0:T(8,128)(2,1)S(1)}, u32[]{:S(2)}, u32[]{:S(2)}) async-start(bf16[128,1,32,256]{3,2,1,0:T(8,128)(2,1)} %bitcast.12), calls=%async_computation | async-start | bytes 4194304 | tf_op jit(solution)/shard_map/all_to_all | solution.py:48
  156.4 1.5 copy-start.1
  157.1 2.3 copy-start
  163.0 3.3 copy-start.2
  163.0 4.9 %copy-start.6 = (bf16[2,512,2,1,128]{4,2,1,3,0:T(2,128)(2,1)S(1)}, bf16[2,512,2,1,128]{4,2,1,3,0:T(2,128)(2,1)}, u32[]{:S(2)}) copy-start(bf16[2,512,2,1,128]{4,2,1,3,0:T(2,128)(2,1)} %get-tuple-element.158) | copy-start | bytes 1572868 | tf_op jit(solution)/shard_map/while
  166.9 1.0 copy-start.3
  168.1 0.8 copy-start.7
  170.5 1.5 copy-start.1
  171.2 2.2 copy-start
  177.1 3.3 copy-start.2
  177.1 4.9 %copy-start.6 = (bf16[2,512,2,1,128]{4,2,1,3,0:T(2,128)(2,1)S(1)}, bf16[2,512,2,1,128]{4,2,1,3,0:T(2,128)(2,1)}, u32[]{:S(2)}) copy-start(bf16[2,512,2,1,128]{4,2,1,3,0:T(2,128)(2,1)} %get-tuple-element.158) | copy-start | bytes 1572868 | tf_op jit(solution)/shard_map/while
  181.0 1.0 copy-start.3
  182.2 0.8 copy-start.7
  296.8 105.9 %copy-start.4 = (bf16[16,32,1,2,128]{4,3,2,1,0:T(2,128)(2,1)S(1)}, bf16[16,32,1,2,128]{4,3,2,1,0:T(2,128)(2,1)}, u32[]{:S(2)}) copy-start(bf16[16,32,1,2,128]{4,3,2,1,0:T(2,128)(2,1)} %param.10) | copy-start | bytes 786436
  296.8 105.9 %copy-start.5 = (f32[16,32,1,2,128]{4,3,2,1,0:T(2,128)S(1)}, f32[16,32,1,2,128]{4,3,2,1,0:T(2,128)}, u32[]{:S(2)}) copy-start(f32[16,32,1,2,128]{4,3,2,1,0:T(2,128)} %param.11) | copy-start | bytes 1572868
where the time goes:
time: 405 us; the launch traced here: 404 us
  blocking collectives  247 us (61%)
  waiting for transfers between devices  99.1 us (24%)
  local copies, waits for them, and re-layouts  19.7 us (5%)
  matrix products  18.8 us (5%)
  starting transfers between devices  10.6 us (3%)
  other arithmetic  7.65 us (2%)
    all_to_all x1, blocking collectives, body(): lax.all_to_all(parcel, ('section', 'doc'), split_axis=0, concat_axis=0, t...  108 us
    psum x1, blocking collectives, body(): lax.psum(jnp.sum(gradient * gradient), ('section', 'doc', 'mp'))  101 us
    all_to_all x1, waiting for transfers between devices, body(): lax.all_to_all(fanned, ('section', 'doc'), split_axis=0, concat_axis=0, t...  99.1 us
    all_gather x1, blocking collectives, body(): lax.all_gather(doc_lists, 'doc', axis=0, tiled=True)  37.9 us
    all_to_all x1, starting transfers between devices, body(): lax.all_to_all(fanned, ('section', 'doc'), split_axis=0, concat_axis=0, t...  10.6 us
  transfers between devices with their start and end apart: 1, of which 1 were waited for; matrix products, arithmetic and copies ran while one was open for 0% of the time, Pallas kernels for 0%

commit v1 on v0

v1 whole, which is shorter than its diff:
```python
import functools
import math

import jax
import jax.numpy as jnp
from jax import lax
from jax.experimental import pallas as pl
from jax.experimental.pallas import tpu as pltpu
from jax.sharding import PartitionSpec as P


momentum_decay = 0.9
step_rate = 0.3
clip_level = 0.5

f32 = jnp.float32
bf16 = jnp.bfloat16
NT = (((1,), (1,)), ((), ()))
NN = (((1,), (0,)), ((), ()))


def dot(a, b, dims):
    return lax.dot_general(a, b, dims, preferred_element_type=f32)


VMEM = pl.BlockSpec(memory_space=pltpu.VMEM)
SMEM = pl.BlockSpec(memory_space=pltpu.SMEM)


def pick_kernel(slot_ref, cache_ref, out_ref, split_ref):
    docs, rows, _ = cache_ref.shape
    half = rows // 2
    row = lax.broadcasted_iota(jnp.int32, (rows, rows), 0)
    col = lax.broadcasted_iota(jnp.int32, (rows, rows), 1)
    source = jnp.where(row < half, 2 * row, 2 * (row - half) + 1)
    order = jnp.where(col == source, 1.0, 0.0).astype(bf16)
    for d in range(docs):
        split_ref[d] = dot(order, cache_ref[d], NN).astype(bf16)

    def one(j, _):
        out_ref[j] = split_ref[jnp.maximum(slot_ref[j, 0, 0], 0)]
        return 0

    lax.fori_loop(0, out_ref.shape[0], one, 0)


def pick(slots, cache):
    readers = slots.shape[0]
    return pl.pallas_call(
        pick_kernel,
        out_shape=jax.ShapeDtypeStruct((readers,) + cache.shape[1:], bf16),
        in_specs=[SMEM, VMEM],
        out_specs=VMEM,
        scratch_shapes=[pltpu.VMEM(cache.shape, bf16)],
        name="pick",
    )(slots, cache)


def load_memory(table_ref, arrived_ref, key_ref, value_ref, r, list_len, part):
    for i in range(list_len):
        o = table_ref[r * list_len + i]
        key_ref[i * part : (i + 1) * part, :] = arrived_ref[o, :part, :]
        value_ref[i * part : (i + 1) * part, :] = arrived_ref[o, part:, :]


def stat_row(table_ref, requests, step, r, t, rows, tiles, sections):
    section = lax.rem(table_ref[requests] + step, sections)
    return (section * rows + r) * tiles + t


def token_refs(refs):
    q_own, t_own, prev, following, q_far, t_far = refs
    qs = (q_own.at[0], prev.at[0, 0], following.at[0, 0], q_far.at[0])
    ts = (t_own.at[0], prev.at[1, 0], following.at[1, 0], t_far.at[0])
    return qs, ts


def token_specs(width, head_size):
    one = pl.BlockSpec((1, width, head_size), lambda r, t: (r, t, 0))
    two = pl.BlockSpec((2, 1, width, head_size), lambda r, t: (0, r, t, 0))
    return one, [one, one, two, two, one, one]


def stats_kernel(list_len, part, scale2, rows, tiles, steps, table_ref, arrived_ref, *refs):
    sections = len(steps)
    q_refs, t_refs = token_refs(refs[:6])
    stats_ref, key_ref, value_ref = refs[6:]
    r, t = pl.program_id(0), pl.program_id(1)
    total = sections * rows * tiles

    @pl.when(t == 0)
    def _():
        load_memory(table_ref, arrived_ref, key_ref, value_ref, r, list_len, part)

    for step, q_ref, t_ref in zip(steps, q_refs, t_refs):
        s = dot(key_ref[...], q_ref[...], NT)
        dp = dot(value_ref[...], t_ref[...], NT)
        top = jnp.max(s, axis=0, keepdims=True)
        p = jnp.exp2((s - top) * scale2)
        index = stat_row(table_ref, rows * list_len, step, r, t, rows, tiles, sections)
        mine = (top, jnp.sum(p, axis=0, keepdims=True), jnp.sum(p * dp, axis=0, keepdims=True))
        for kind, value in enumerate(mine):
            for c in range(sections):
                stats_ref[c, pl.ds(kind * total + index, 1), :] = value


def grad_kernel(list_len, part, scale, scale2, rows, tiles, steps, table_ref, arrived_ref, stats_ref, *refs):
    sections = len(steps)
    q_refs, t_refs = token_refs(refs[:6])
    out_refs = refs[6 : 6 + sections]
    parcel_ref, key_ref, value_ref, turned_ref, total_ref, dk_ref, dv_ref = refs[6 + sections :]
    r, t = pl.program_id(0), pl.program_id(1)
    total = sections * rows * tiles

    @pl.when((r == 0) & (t == 0))
    def _():
        parcel_ref[...] = jnp.zeros_like(parcel_ref)
        tops = [stats_ref[c, :total, :] for c in range(sections)]
        top = functools.reduce(jnp.maximum, tops)
        shares = [jnp.exp2((x - top) * scale2) for x in tops]
        norm = sum(a * stats_ref[c, total : 2 * total, :] for c, a in enumerate(shares))
        dots = sum(a * stats_ref[c, 2 * total :, :] for c, a in enumerate(shares))
        inverse = 1.0 / norm
        total_ref[:total, :] = top
        total_ref[total : 2 * total, :] = inverse
        total_ref[2 * total :, :] = dots * inverse

    @pl.when(t == 0)
    def _():
        load_memory(table_ref, arrived_ref, key_ref, value_ref, r, list_len, part)
        turned_ref[...] = value_ref[...].astype(f32).T.astype(bf16)
        dk_ref[...] = jnp.zeros_like(dk_ref)
        dv_ref[...] = jnp.zeros_like(dv_ref)

    for step, q_ref, t_ref, out_ref in zip(steps, q_refs, t_refs, out_refs):
        q, tangent = q_ref[...], t_ref[...]
        index = stat_row(table_ref, rows * list_len, step, r, t, rows, tiles, sections)
        top = total_ref[pl.ds(index, 1), :]
        inverse = total_ref[pl.ds(total + index, 1), :]
        delta = total_ref[pl.ds(2 * total + index, 1), :]
        s = dot(key_ref[...], q, NT)
        w = jnp.exp2((s - top) * scale2) * inverse
        w16 = w.astype(bf16)
        out_ref[0] = dot(turned_ref[...], w16, NN).T.astype(bf16)
        dv_ref[...] += dot(w16, tangent, NN)
        dp = dot(value_ref[...], tangent, NT)
        ds = (w * (dp - delta)).astype(bf16)
        dk_ref[...] += dot(ds, q, NN)

    @pl.when(t == tiles - 1)
    def _():
        for i in range(list_len):
            o = table_ref[r * list_len + i]
            parcel_ref[o, :part, :] = (dk_ref[i * part : (i + 1) * part, :] * scale).astype(bf16)
            parcel_ref[o, part:, :] = dv_ref[i * part : (i + 1) * part, :].astype(bf16)


def row_stats(table, arrived, tensors, steps, list_len, part, width):
    rows, tokens, head_size = tensors[0].shape
    tiles, keys, sections = tokens // width, list_len * part, len(steps)
    _, token_ins = token_specs(width, head_size)
    scale2 = math.log2(math.e) / math.sqrt(head_size)
    pairs = rows * sections * tokens * keys
    return pl.pallas_call(
        functools.partial(stats_kernel, list_len, part, scale2, rows, tiles, steps),
        out_shape=jax.ShapeDtypeStruct((sections, 3 * sections * rows * tiles, width), f32),
        grid=(rows, tiles),
        in_specs=[SMEM, VMEM] + token_ins,
        out_specs=VMEM,
        scratch_shapes=[pltpu.VMEM((keys, head_size), bf16)] * 2,
        cost_estimate=pl.CostEstimate(
            flops=4 * pairs * head_size, bytes_accessed=4 * sections * tensors[0].size, transcendentals=pairs
        ),
        name="stats",
    )(table, arrived, *tensors)


def row_grads(table, arrived, stats, tensors, steps, list_len, part, width):
    rows, tokens, head_size = tensors[0].shape
    tiles, keys, sections = tokens // width, list_len * part, len(steps)
    spec, token_ins = token_specs(width, head_size)
    scale = 1.0 / math.sqrt(head_size)
    scale2 = math.log2(math.e) * scale
    pairs = rows * sections * tokens * keys
    return pl.pallas_call(
        functools.partial(grad_kernel, list_len, part, scale, scale2, rows, tiles, steps),
        out_shape=[jax.ShapeDtypeStruct(tensors[0].shape, bf16)] * sections + [jax.ShapeDtypeStruct(arrived.shape, bf16)],
        grid=(rows, tiles),
        in_specs=[SMEM, VMEM, VMEM] + token_ins,
        out_specs=[spec] * sections + [VMEM],
        scratch_shapes=[
            pltpu.VMEM((keys, head_size), bf16),
            pltpu.VMEM((keys, head_size), bf16),
            pltpu.VMEM((head_size, keys), bf16),
            pltpu.VMEM(stats.shape[1:], f32),
            pltpu.VMEM((keys, head_size), f32),
            pltpu.VMEM((keys, head_size), f32),
        ],
        cost_estimate=pl.CostEstimate(
            flops=10 * pairs * head_size, bytes_accessed=6 * sections * tensors[0].size, transcendentals=pairs
        ),
        name="grads",
    )(table, arrived, stats, *tensors)


def collect_kernel(slot_ref, returned_ref, grad_ref, square_ref):
    grad_ref[...] = jnp.zeros_like(grad_ref)

    def one(j, _):
        @pl.when(slot_ref[j, 0, 0] >= 0)
        def _():
            d = slot_ref[j, 0, 0]
            grad_ref[d] = grad_ref[d] + returned_ref[j].astype(f32)

        return 0

    lax.fori_loop(0, returned_ref.shape[0], one, 0)

    def square(d, total):
        g = grad_ref[d]
        return total + g * g

    total = lax.fori_loop(0, grad_ref.shape[0], square, jnp.zeros(grad_ref.shape[1:], f32))
    total = jnp.sum(total, axis=0, keepdims=True)
    for j in range(square_ref.shape[0]):
        square_ref[j] = total


def collect(slots, returned, docs):
    return pl.pallas_call(
        collect_kernel,
        out_shape=(
            jax.ShapeDtypeStruct((docs,) + returned.shape[1:], f32),
            jax.ShapeDtypeStruct((returned.shape[0], 1, returned.shape[2]), f32),
        ),
        in_specs=[SMEM, VMEM],
        out_specs=(VMEM, VMEM),
        name="collect",
    )(slots, returned)


def fold_kernel(square_ref, out_ref):
    total = functools.reduce(jnp.add, [square_ref[j] for j in range(square_ref.shape[0])])
    for j in range(out_ref.shape[0]):
        out_ref[j] = total


def fold(square, count):
    return pl.pallas_call(
        fold_kernel,
        out_shape=jax.ShapeDtypeStruct((count,) + square.shape[1:], f32),
        in_specs=[VMEM],
        out_specs=VMEM,
        name="fold",
    )(square)


def update_kernel(clip_limit, square_ref, grad_ref, cache_ref, momentum_ref, new_cache_ref, new_momentum_ref):
    total = functools.reduce(jnp.add, [square_ref[j] for j in range(square_ref.shape[0])])
    norm = jnp.sqrt(jnp.sum(total, axis=1, keepdims=True))
    factor = clip_limit / jnp.maximum(norm, clip_limit)
    docs, rows, _ = grad_ref.shape
    half = rows // 2

    def one(d, _):
        for kind in range(2):
            at = (d, pl.ds(kind, half, stride=2), slice(None))
            new_momentum_ref[at] = momentum_decay * momentum_ref[at] + factor * grad_ref[d, kind * half : (kind + 1) * half, :]
        new_cache_ref[d] = (cache_ref[d].astype(f32) - step_rate * new_momentum_ref[d]).astype(bf16)
        return 0

    lax.fori_loop(0, docs, one, 0)


def update(clip_limit, square, grad, cache, momentum):
    return pl.pallas_call(
        functools.partial(update_kernel, clip_limit),
        out_shape=(jax.ShapeDtypeStruct(cache.shape, bf16), jax.ShapeDtypeStruct(momentum.shape, f32)),
        in_specs=[VMEM] * 4,
        out_specs=(VMEM, VMEM),
        name="update",
    )(square, grad, cache, momentum)


def swap(x, axes):
    return lax.all_to_all(x, axes, split_axis=0, concat_axis=0, tiled=True)


def pass_on(x, ring):
    return lax.ppermute(x, "section", ring)


def body(queries, cotangent, cache, momentum, doc_lists, place):
    rows_dev, seq_len, head_count, kv_count, head_size = queries.shape
    doc_dev, len_part = cache.shape[:2]
    doc_total = place.shape[0]
    owners = doc_total // doc_dev
    list_len = doc_lists.shape[1]
    requests = rows_dev * list_len
    sections = lax.axis_size("section")
    tokens = seq_len * head_count

    q_own = queries.reshape(rows_dev, tokens, head_size)
    t_own = cotangent.reshape(rows_dev, tokens, head_size)
    up = [(i, (i + 1) % sections) for i in range(sections)]
    down = [(i, (i - 1) % sections) for i in range(sections)]
    across = [(i, (i + 2) % sections) for i in range(sections)]
    both = jnp.stack([q_own, t_own])
    prev, following = pass_on(both, up), pass_on(both, down)
    q_far, t_far = pass_on(prev[0], up), pass_on(following[1], down)
    tensors = (q_own, t_own, prev, following, q_far, t_far)
    steps = (0, 3, 1, 2)

    lists = doc_lists.reshape(requests)
    named = lists[:, None] == jnp.arange(doc_total, dtype=jnp.int32)[None, :]
    positions = jnp.sum(jnp.where(named, place[None, :], 0), axis=1)
    holder = positions // doc_dev
    wanted = jnp.sum(
        jnp.where(holder[None, :] == jnp.arange(owners, dtype=jnp.int32)[:, None], positions[None, :] % doc_dev + 1, 0),
        axis=1,
    ) - 1
    slots = swap(wanted.reshape(owners, 1, 1), "doc")

    stored = cache.reshape(doc_dev, len_part * 2, head_size)
    outgoing = pick(slots, stored)
    arrived = swap(outgoing, "doc")

    width = 512
    table = jnp.concatenate([holder, lax.axis_index("section").reshape(1).astype(jnp.int32)])
    stats = swap(row_stats(table, arrived, tensors, steps, list_len, len_part, width), "section")
    own, to_prev, to_next, to_far, parcel = row_grads(table, arrived, stats, tensors, steps, list_len, len_part, width)
    shares = (own, pass_on(to_prev, down), pass_on(to_next, up), pass_on(to_far, across))
    attention = sum(x.astype(f32) for x in shares).astype(bf16).reshape(queries.shape)

    returned = swap(parcel, "doc")
    gradient, square = collect(slots, returned, doc_dev)
    planes = sections * lax.axis_size("mp")
    square = fold(swap(square, "doc"), planes)
    square = swap(square, ("section", "mp"))
    entry_count = doc_total * len_part * planes * kv_count * 2 * head_size
    clip_limit = clip_level * math.sqrt(entry_count)
    new_cache, new_momentum = update(
        clip_limit, square, gradient, stored, momentum.reshape(doc_dev, len_part * 2, head_size)
    )
    return (attention, new_cache.reshape(cache.shape), new_momentum.reshape(momentum.shape))


def solution(mesh):
    in_specs = (
        P("doc", None, "section", "mp", None),
        P("doc", None, "section", "mp", None),
        P("doc", "section", "mp", None, None),
        P("doc", "section", "mp", None, None),
        P("doc", None),
        P(),
    )
    out_specs = (
        P("doc", None, "section", "mp", None),
        P("doc", "section", "mp", None, None),
        P("doc", "section", "mp", None, None),
    )

    return jax.shard_map(body, mesh=mesh, in_specs=in_specs, out_specs=out_specs, check_vma=False)
```

time: 405 us -> 202 us (0.50)
  blocking collectives: 247 us -> 54.7 us
  starting transfers between devices: 10.6 us -> 45.9 us
  waiting for transfers between devices: 99.1 us -> 65.1 us
  Pallas kernels: 0 us -> 27.1 us
  matrix products: 18.8 us -> 0 us
  local copies, waits for them, and re-layouts: 19.7 us -> 3.31 us
    psum x1 -> x0, blocking collectives: 101 us -> none  [body(): lax.psum(jnp.sum(gradient * gradient), ('section', 'doc', 'mp'))]
    all_to_all x1 -> x3, waiting for transfers between devices: 99.1 us -> 30.8 us  [swap(): return lax.all_to_all(x, axes, split_axis=0, concat_axis=0, tiled=True)]
    all_to_all x1 -> x3, blocking collectives: 108 us -> 54.7 us  [swap(): return lax.all_to_all(x, axes, split_axis=0, concat_axis=0, tiled=True)]
    all_gather x1 -> x0, blocking collectives: 37.9 us -> none  [body(): lax.all_gather(doc_lists, 'doc', axis=0, tiled=True)]
    ppermute x0 -> x7, waiting for transfers between devices: none -> 34.3 us  [pass_on(): return lax.ppermute(x, 'section', ring)]
    pallas_call x0 -> x6, Pallas kernels: none -> 27.1 us  [the longest x1 12.4 us: row_grads(): pl.pallas_call(functools.partial(grad_kernel, list_len, part, scale, scal...]
    ppermute x0 -> x7, starting transfers between devices: none -> 21.5 us  [pass_on(): return lax.ppermute(x, 'section', ring)]
    dot_general x9 -> x0, matrix products: 18.8 us -> none  [the longest x2 7.19 us: row_attention(): jnp.einsum('qk,qd->kd', grad_scores, query, preferred_element_type=jnp.fl...]
  transfers between devices with their start and end apart: 1 -> 10, of which waited for: 1 -> 4; matrix products, arithmetic and copies ran while one was open for 0% -> 2% of each run, Pallas kernels for 0% -> 3%
where the time goes in v1:
time: 202 us; the launch traced here: 201 us
  waiting for transfers between devices  65.1 us (32%)
  blocking collectives  54.7 us (27%)
  starting transfers between devices  45.9 us (23%)
  Pallas kernels  27.1 us (13%)
  other arithmetic  4.24 us (2%)
  local copies, waits for them, and re-layouts  3.31 us (2%)
    all_to_all x3, blocking collectives, swap(): return lax.all_to_all(x, axes, split_axis=0, concat_axis=0, tiled=True)  54.7 us
    ppermute x7, waiting for transfers between devices, pass_on(): return lax.ppermute(x, 'section', ring)  34.3 us
    all_to_all x3, waiting for transfers between devices, swap(): return lax.all_to_all(x, axes, split_axis=0, concat_axis=0, tiled=True)  30.8 us
    all_to_all x3, starting transfers between devices, swap(): return lax.all_to_all(x, axes, split_axis=0, concat_axis=0, tiled=True)  24.4 us
    ppermute x7, starting transfers between devices, pass_on(): return lax.ppermute(x, 'section', ring)  21.5 us
    pallas_call x1, Pallas kernels, row_grads(): pl.pallas_call(functools.partial(grad_kernel, list_len, part, scale, scal...  12.4 us
    pallas_call x1, Pallas kernels, row_stats(): pl.pallas_call(functools.partial(stats_kernel, list_len, part, scale2, ro...  6.2 us
  transfers between devices with their start and end apart: 10, of which 4 were waited for; matrix products, arithmetic and copies ran while one was open for 2% of the time, Pallas kernels for 3%

profile of v1, /device:TPU:1, one launch (start us, length us, event | category | flops | bytes accessed | tf_op | source)
XLA Modules:
  0.0 201.2 jit_solution(14305052894061558912)
XLA Ops:
  0.7 2.3 %pad_maximum_fusion = bf16[2,2,1024,128]{3,2,1,0:T(8,128)(2,1)} fusion(bf16[1,2,1024,128]{3,2,1,0:T(8,128)(2,1)} %bitcast.25, bf16[1,2,1024,128]{3,2,1,0:T(8,128)(2,1)} %bitcast.22), kind=kLoop, calls=%fused_computation | loop fusion | flops 524288 | bytes 2097152 | tf_op jit(solution)/shard_map/stack | solution.py:308
  2.9 5.2 %collective-permute-start.1 = (bf16[2,2,1024,128]{3,2,1,0:T(8,128)(2,1)}, bf16[2,2,1024,128]{3,2,1,0:T(8,128)(2,1)S(1)}, u32[]{:S(2)}, u32[]{:S(2)}) collective-permute-start(bf16[2,2,1024,128]{3,2,1,0:T(8,128)(2,1)} %pad_maximum_fusion), channel_id=1, source_target_pairs={{0,384},{128,0},{256,128},{384,256},{1,385},{129,1},{257,129},{385... | collective-permute-start | bytes 3145736 | tf_op jit(solution)/shard_map/ppermute | solution.py:290
  8.6 27.9 %all_to_all.30.slot_ref = s32[32,1,1]{2,1,0:T(1,128)} all-to-all(s32[32,1,1]{2,1,0:T(1,128)S(1)} %copy.13), channel_id=1, replica_groups=mesh['section'=4,'doc'=32,'mp'=4] {'doc'}, dimensions={0} | all-to-all | bytes 256 | tf_op jit(solution)/shard_map/all_to_all | solution.py:286
  36.5 2.2 %pick.1 = bf16[32,64,128]{2,1,0:T(8,128)(2,1)} custom-call(s32[32,1,1]{2,1,0:T(1,128)} %all_to_all.30.slot_ref, bf16[16,64,128]{2,1,0:T(8,128)(2,1)} %bitcast.28), custom_call_target="tpu_custom_call" | custom-call | tf_op jit(solution)/shard_map/pick/pallas_call | solution.py:49
  38.8 4.3 %all-to-all-start.1 = ((bf16[32,64,128]{2,1,0:T(8,128)(2,1)}), bf16[32,64,128]{2,1,0:T(8,128)(2,1)S(1)}, u32[]{:S(2)}, u32[]{:S(2)}) async-start(bf16[32,64,128]{2,1,0:T(8,128)(2,1)} %pick.1), calls=%async_computation.1 | async-start | bytes 1048576 | tf_op jit(solution)/shard_map/all_to_all | solution.py:286
  43.1 1.9 collective-permute-start
  45.0 4.6 %collective-permute-start.3 = (bf16[2,1024,128]{2,1,0:T(8,128)(2,1)S(1)}, bf16[2,1024,128]{2,1,0:T(8,128)(2,1)}, u32[]{:S(2)}, u32[]{:S(2)}) collective-permute-start(bf16[2,1024,128]{2,1,0:T(8,128)(2,1)S(1)} %slice_bitcast_fusion), channel_id=1, source_target_pairs={{0,384},{128,0},{256,128},{384,256},{1,385},{129,1},{257,129},{385... | collective-permute-start | bytes 1572872 | tf_op jit(solution)/shard_map/ppermute | solution.py:290
  49.6 21.1 %collective-permute-done.refs_2_ = bf16[2,2,1024,128]{3,2,1,0:T(8,128)(2,1)S(1)} collective-permute-done((bf16[2,2,1024,128]{3,2,1,0:T(8,128)(2,1)}, bf16[2,2,1024,128]{3,2,1,0:T(8,128)(2,1)S(1)}, u32[]{:S(2)}, u32[]{:S(2)}) %collective-permute-start) | collective-permute-done | bytes 1048608 | tf_op jit(solution)/shard_map/ppermute | solution.py:290
  71.6 1.9 collective-permute-start.2
  74.2 13.2 %collective-permute-done.2.refs_4_ = bf16[2,1024,128]{2,1,0:T(8,128)(2,1)} collective-permute-done((bf16[2,1024,128]{2,1,0:T(8,128)(2,1)}, bf16[2,1024,128]{2,1,0:T(8,128)(2,1)}, u32[]{:S(2)}, u32[]{:S(2)}) %collective-permute-start.2) | collective-permute-done | bytes 524320 | tf_op jit(solution)/shard_map/ppermute | solution.py:290
  88.1 6.2 %stats.1 = f32[4,48,512]{2,1,0:T(8,128)} custom-call(s32[17]{0:T(128)} %pad_add_fusion.table_ref, bf16[32,64,128]{2,1,0:T(8,128)(2,1)} %copy-done.3, bf16[2,1024,128]{2,1,0:T(8,128)(2,1)} %bitcast.23, bf16[2,1024,128]{2,1,0:T(8,128)(2,1)} %bitcast.26, bf16[2,2,1024,128]{3,2,1,0:T(8,128)(2,1)} %copy-done.1, bf16[2,2,1024,128]{3,2,1,0:T(8,128)(2,1)} %copy-done, ...), custom_call_target="tpu_custom_call" | custom-call | flops 1073741824 | bytes 4194304 | tf_op jit(solution)/shard_map/stats/pallas_call | solution.py:164
  94.3 10.4 %all_to_all.31.stats_ref = f32[4,48,512]{2,1,0:T(8,128)} all-to-all(f32[4,48,512]{2,1,0:T(8,128)} %stats.1), channel_id=1, replica_groups=mesh['section'=4,'doc'=32,'mp'=4] {'section'}, dimensions={0} | all-to-all | bytes 786432 | tf_op jit(solution)/shard_map/all_to_all | solution.py:286
  104.7 12.4 %grads.1 = (bf16[2,1024,128]{2,1,0:T(8,128)(2,1)}, bf16[2,1024,128]{2,1,0:T(8,128)(2,1)}, bf16[2,1024,128]{2,1,0:T(8,128)(2,1)}, bf16[2,1024,128]{2,1,0:T(8,128)(2,1)}, bf16[32,64,128]{2,1,0:T(8,128)(2,1)}) custom-call(s32[17]{0:T(128)} %pad_add_fusion.table_ref, bf16[32,64,128]{2,1,0:T(8,128)(2,1)} %copy-done.3, f32[4,48,512]{2,1,0:T(8,128)} %all_to_all.31.stats_ref, ...), custom_call_target="tpu_custom_call" | custom-call | flops 2684354560 | bytes 6291456 | tf_op jit(solution)/shard_map/grads/pallas_call | solution.py:185
  117.1 15.2 %all-to-all-start.3 = ((bf16[32,64,128]{2,1,0:T(8,128)(2,1)}), bf16[32,64,128]{2,1,0:T(8,128)(2,1)S(1)}, u32[]{:S(2)}, u32[]{:S(2)}) async-start(bf16[32,64,128]{2,1,0:T(8,128)(2,1)} %get-tuple-element.16), calls=%async_computation.3 | async-start | bytes 1048576 | tf_op jit(solution)/shard_map/all_to_all | solution.py:286
  132.4 2.9 %collective-permute-start.4 = (bf16[2,1024,128]{2,1,0:T(8,128)(2,1)}, bf16[2,1024,128]{2,1,0:T(8,128)(2,1)S(1)}, u32[]{:S(2)}, u32[]{:S(2)}) collective-permute-start(bf16[2,1024,128]{2,1,0:T(8,128)(2,1)} %get-tuple-element.13), channel_id=1, source_target_pairs={{0,384},{128,0},{256,128},{384,256},{1,385},{129,1},{257,129},{385... | collective-permute-start | bytes 1572872 | tf_op jit(solution)/shard_map/ppermute | solution.py:290
  135.3 2.5 %collective-permute-start.5 = (bf16[2,1024,128]{2,1,0:T(8,128)(2,1)}, bf16[2,1024,128]{2,1,0:T(8,128)(2,1)S(1)}, u32[]{:S(2)}, u32[]{:S(2)}) collective-permute-start(bf16[2,1024,128]{2,1,0:T(8,128)(2,1)} %get-tuple-element.14), channel_id=1, source_target_pairs={{0,128},{128,256},{256,384},{384,0},{1,129},{129,257},{257,385},{3... | collective-permute-start | bytes 1572872 | tf_op jit(solution)/shard_map/ppermute | solution.py:290
  137.8 2.5 %collective-permute-start.6 = (bf16[2,1024,128]{2,1,0:T(8,128)(2,1)S(1)}, bf16[2,1024,128]{2,1,0:T(8,128)(2,1)S(1)}, u32[]{:S(2)}, u32[]{:S(2)}) collective-permute-start(bf16[2,1024,128]{2,1,0:T(8,128)(2,1)S(1)} %copy-done.7), channel_id=1, source_target_pairs={{0,256},{128,384},{256,0},{384,128},{1,257},{129,385},{257,1},{385... | collective-permute-start | bytes 1572872 | tf_op jit(solution)/shard_map/ppermute | solution.py:290
  140.3 25.5 %all-to-all-done.3.returned_ref = bf16[32,64,128]{2,1,0:T(8,128)(2,1)S(1)} async-done(((bf16[32,64,128]{2,1,0:T(8,128)(2,1)}), bf16[32,64,128]{2,1,0:T(8,128)(2,1)S(1)}, u32[]{:S(2)}, u32[]{:S(2)}) %all-to-all-start.3) | async-done | bytes 524320 | tf_op jit(solution)/shard_map/all_to_all | solution.py:286
  166.7 2.5 %collect.1 = (f32[16,64,128]{2,1,0:T(8,128)}, f32[32,1,128]{2,1,0:T(1,128)}) custom-call(s32[32,1,1]{2,1,0:T(1,128)} %all_to_all.30.slot_ref, bf16[32,64,128]{2,1,0:T(8,128)(2,1)} %copy-done.2), custom_call_target="tpu_custom_call" | custom-call | tf_op jit(solution)/shard_map/collect/pallas_call | solution.py:230
  169.1 16.3 %all_to_all.32.square_ref = f32[32,1,128]{2,1,0:T(1,128)} all-to-all(f32[32,1,128]{2,1,0:T(1,128)} %get-tuple-element.17), channel_id=1, replica_groups=mesh['section'=4,'doc'=32,'mp'=4] {'doc'}, dimensions={0} | all-to-all | bytes 32768 | tf_op jit(solution)/shard_map/all_to_all | solution.py:286
  185.4 1.4 fold.1
  186.8 4.9 %all-to-all-start.5 = ((f32[16,1,128]{2,1,0:T(1,128)}), f32[16,1,128]{2,1,0:T(1,128)S(1)}, u32[]{:S(2)}, u32[]{:S(2)}) async-start(f32[16,1,128]{2,1,0:T(1,128)} %fold.1), calls=%async_computation.5 | async-start | bytes 16384 | tf_op jit(solution)/shard_map/all_to_all | solution.py:286
  192.8 5.3 %all-to-all-done.5.square_ref = f32[16,1,128]{2,1,0:T(1,128)S(1)} async-done(((f32[16,1,128]{2,1,0:T(1,128)}), f32[16,1,128]{2,1,0:T(1,128)S(1)}, u32[]{:S(2)}, u32[]{:S(2)}) %all-to-all-start.5) | async-done | bytes 8224 | tf_op jit(solution)/shard_map/all_to_all | solution.py:286
  198.7 2.5 %update.1 = (bf16[16,64,128]{2,1,0:T(8,128)(2,1)}, f32[16,64,128]{2,1,0:T(8,128)}) custom-call(f32[16,1,128]{2,1,0:T(1,128)} %copy-done.5, f32[16,64,128]{2,1,0:T(8,128)} %get-tuple-element.18.grad_ref, bf16[16,64,128]{2,1,0:T(8,128)(2,1)} %bitcast.29, f32[16,64,128]{2,1,0:T(8,128)} %bitcast.31), custom_call_target="tpu_custom_call" | custom-call | tf_op jit(solution)/shard_map/update/pallas_call | solution.py:276
  (34 shorter events, 5.3 us)
Async XLA Ops:
  0.6 7.5 %copy-start.8 = (s32[2,8]{1,0:T(2,128)S(1)}, s32[2,8]{1,0:T(2,128)}, u32[]{:S(2)}) copy-start(s32[2,8]{1,0:T(2,128)} %param.10) | copy-start | bytes 196
  0.6 7.6 %copy-start.6 = (s32[512]{0:T(512)S(1)}, s32[512]{0:T(512)}, u32[]{:S(2)}) copy-start(s32[512]{0:T(512)} %param.11) | copy-start | bytes 6148
  2.9 42.1 %collective-permute-start.1 = (bf16[2,2,1024,128]{3,2,1,0:T(8,128)(2,1)}, bf16[2,2,1024,128]{3,2,1,0:T(8,128)(2,1)S(1)}, u32[]{:S(2)}, u32[]{:S(2)}) collective-permute-start(bf16[2,2,1024,128]{3,2,1,0:T(8,128)(2,1)} %pad_maximum_fusion), channel_id=1, source_target_pairs={{0,384},{128,0},{256,128},{384,256},{1,385},{129,1},{257,129},{385... | collective-permute-start | bytes 3145736 | tf_op jit(solution)/shard_map/ppermute | solution.py:290
  38.8 48.6 %all-to-all-start.1 = ((bf16[32,64,128]{2,1,0:T(8,128)(2,1)}), bf16[32,64,128]{2,1,0:T(8,128)(2,1)S(1)}, u32[]{:S(2)}, u32[]{:S(2)}) async-start(bf16[32,64,128]{2,1,0:T(8,128)(2,1)} %pick.1), calls=%async_computation.1 | async-start | bytes 1048576 | tf_op jit(solution)/shard_map/all_to_all | solution.py:286
  43.1 27.7 %collective-permute-start = (bf16[2,2,1024,128]{3,2,1,0:T(8,128)(2,1)}, bf16[2,2,1024,128]{3,2,1,0:T(8,128)(2,1)S(1)}, u32[]{:S(2)}, u32[]{:S(2)}) collective-permute-start(bf16[2,2,1024,128]{3,2,1,0:T(8,128)(2,1)} %pad_maximum_fusion), channel_id=1, source_target_pairs={{0,128},{128,256},{256,384},{384,0},{1,129},{129,257},{257,385},{3... | collective-permute-start | bytes 3145736 | tf_op jit(solution)/shard_map/ppermute | solution.py:290
  45.0 28.6 %copy-start = (bf16[2,2,1024,128]{3,2,1,0:T(8,128)(2,1)}, bf16[2,2,1024,128]{3,2,1,0:T(8,128)(2,1)S(1)}, u32[]{:S(2)}) copy-start(bf16[2,2,1024,128]{3,2,1,0:T(8,128)(2,1)S(1)} %collective-permute-done.1.refs_3_) | copy-start | bytes 3145732
  45.0 29.1 %collective-permute-start.3 = (bf16[2,1024,128]{2,1,0:T(8,128)(2,1)S(1)}, bf16[2,1024,128]{2,1,0:T(8,128)(2,1)}, u32[]{:S(2)}, u32[]{:S(2)}) collective-permute-start(bf16[2,1024,128]{2,1,0:T(8,128)(2,1)S(1)} %slice_bitcast_fusion), channel_id=1, source_target_pairs={{0,384},{128,0},{256,128},{384,256},{1,385},{129,1},{257,129},{385... | collective-permute-start | bytes 1572872 | tf_op jit(solution)/shard_map/ppermute | solution.py:290
  70.7 16.6 %copy-start.1 = (bf16[2,2,1024,128]{3,2,1,0:T(8,128)(2,1)}, bf16[2,2,1024,128]{3,2,1,0:T(8,128)(2,1)S(1)}, u32[]{:S(2)}) copy-start(bf16[2,2,1024,128]{3,2,1,0:T(8,128)(2,1)S(1)} %collective-permute-done.refs_2_) | copy-start | bytes 3145732
  71.6 15.7 %collective-permute-start.2 = (bf16[2,1024,128]{2,1,0:T(8,128)(2,1)}, bf16[2,1024,128]{2,1,0:T(8,128)(2,1)}, u32[]{:S(2)}, u32[]{:S(2)}) collective-permute-start(bf16[2,1024,128]{2,1,0:T(8,128)(2,1)} %slice_bitcast_fusion.1), channel_id=1, source_target_pairs={{0,128},{128,256},{256,384},{384,0},{1,129},{129,257},{257,385},{3... | collective-permute-start | bytes 1572872 | tf_op jit(solution)/shard_map/ppermute | solution.py:290
  87.3 0.8 copy-start.3
  117.1 20.7 %copy-start.7 = (bf16[2,1024,128]{2,1,0:T(8,128)(2,1)S(1)}, bf16[2,1024,128]{2,1,0:T(8,128)(2,1)}, u32[]{:S(2)}) copy-start(bf16[2,1024,128]{2,1,0:T(8,128)(2,1)} %get-tuple-element.15) | copy-start | bytes 1572868
  117.1 48.7 %all-to-all-start.3 = ((bf16[32,64,128]{2,1,0:T(8,128)(2,1)}), bf16[32,64,128]{2,1,0:T(8,128)(2,1)S(1)}, u32[]{:S(2)}, u32[]{:S(2)}) async-start(bf16[32,64,128]{2,1,0:T(8,128)(2,1)} %get-tuple-element.16), calls=%async_computation.3 | async-start | bytes 1048576 | tf_op jit(solution)/shard_map/all_to_all | solution.py:286
  132.3 59.4 %copy-start.4 = (bf16[2,1024,128]{2,1,0:T(8,128)(2,1)S(1)}, bf16[2,1024,128]{2,1,0:T(8,128)(2,1)}, u32[]{:S(2)}) copy-start(bf16[2,1024,128]{2,1,0:T(8,128)(2,1)} %get-tuple-element.12) | copy-start | bytes 1572868
  132.4 59.4 %collective-permute-start.4 = (bf16[2,1024,128]{2,1,0:T(8,128)(2,1)}, bf16[2,1024,128]{2,1,0:T(8,128)(2,1)S(1)}, u32[]{:S(2)}, u32[]{:S(2)}) collective-permute-start(bf16[2,1024,128]{2,1,0:T(8,128)(2,1)} %get-tuple-element.13), channel_id=1, source_target_pairs={{0,384},{128,0},{256,128},{384,256},{1,385},{129,1},{257,129},{385... | collective-permute-start | bytes 1572872 | tf_op jit(solution)/shard_map/ppermute | solution.py:290
  135.3 56.4 %collective-permute-start.5 = (bf16[2,1024,128]{2,1,0:T(8,128)(2,1)}, bf16[2,1024,128]{2,1,0:T(8,128)(2,1)S(1)}, u32[]{:S(2)}, u32[]{:S(2)}) collective-permute-start(bf16[2,1024,128]{2,1,0:T(8,128)(2,1)} %get-tuple-element.14), channel_id=1, source_target_pairs={{0,128},{128,256},{256,384},{384,0},{1,129},{129,257},{257,385},{3... | collective-permute-start | bytes 1572872 | tf_op jit(solution)/shard_map/ppermute | solution.py:290
  137.8 53.9 %collective-permute-start.6 = (bf16[2,1024,128]{2,1,0:T(8,128)(2,1)S(1)}, bf16[2,1024,128]{2,1,0:T(8,128)(2,1)S(1)}, u32[]{:S(2)}, u32[]{:S(2)}) collective-permute-start(bf16[2,1024,128]{2,1,0:T(8,128)(2,1)S(1)} %copy-done.7), channel_id=1, source_target_pairs={{0,256},{128,384},{256,0},{384,128},{1,257},{129,385},{257,1},{385... | collective-permute-start | bytes 1572872 | tf_op jit(solution)/shard_map/ppermute | solution.py:290
  165.9 0.8 copy-start.2
  186.8 11.3 %all-to-all-start.5 = ((f32[16,1,128]{2,1,0:T(1,128)}), f32[16,1,128]{2,1,0:T(1,128)S(1)}, u32[]{:S(2)}, u32[]{:S(2)}) async-start(f32[16,1,128]{2,1,0:T(1,128)} %fold.1), calls=%async_computation.5 | async-start | bytes 16384 | tf_op jit(solution)/shard_map/all_to_all | solution.py:286
  198.1 0.6 copy-start.5

commit v2 on v1

v2 whole, which is shorter than its diff:
```python
import functools
import math

import jax
import jax.numpy as jnp
from jax import lax
from jax.experimental import pallas as pl
from jax.experimental.pallas import tpu as pltpu
from jax.sharding import PartitionSpec as P


momentum_decay = 0.9
step_rate = 0.3
clip_level = 0.5

f32 = jnp.float32
bf16 = jnp.bfloat16
NT = (((1,), (1,)), ((), ()))
NN = (((1,), (0,)), ((), ()))


def dot(a, b, dims):
    return lax.dot_general(a, b, dims, preferred_element_type=f32)


VMEM = pl.BlockSpec(memory_space=pltpu.VMEM)
SMEM = pl.BlockSpec(memory_space=pltpu.SMEM)


def small(mib):
    return pltpu.CompilerParams(vmem_limit_bytes=mib << 20)


def ask_kernel(doc_dev, list_ref, place_ref, wanted_ref, table_ref):
    for o in range(wanted_ref.shape[0]):
        wanted_ref[o, 0, 0] = -1
    rows, list_len = list_ref.shape
    for i in range(rows * list_len):
        position = place_ref[list_ref[i // list_len, i % list_len]]
        holder = lax.div(position, doc_dev)
        table_ref[i] = holder
        wanted_ref[holder, 0, 0] = lax.rem(position, doc_dev)
    table_ref[rows * list_len] = lax.axis_index("section").astype(jnp.int32)


def ask(doc_lists, place, owners, doc_dev):
    return pl.pallas_call(
        functools.partial(ask_kernel, doc_dev),
        out_shape=(
            jax.ShapeDtypeStruct((owners, 1, 1), jnp.int32),
            jax.ShapeDtypeStruct((doc_lists.size + 1,), jnp.int32),
        ),
        in_specs=[SMEM, SMEM],
        out_specs=(SMEM, SMEM),
        name="ask",
    )(doc_lists, place)


def split_kernel(cache_ref, split_ref):
    docs, rows, _ = cache_ref.shape
    half = rows // 2
    row = lax.broadcasted_iota(jnp.int32, (rows, rows), 0)
    col = lax.broadcasted_iota(jnp.int32, (rows, rows), 1)
    source = jnp.where(row < half, 2 * row, 2 * (row - half) + 1)
    order = jnp.where(col == source, 1.0, 0.0).astype(bf16)
    for d in range(docs):
        split_ref[d] = dot(order, cache_ref[d], NN).astype(bf16)


def split(cache):
    return pl.pallas_call(
        split_kernel,
        out_shape=jax.ShapeDtypeStruct(cache.shape, bf16),
        in_specs=[VMEM],
        out_specs=VMEM,
        compiler_params=small(4),
        name="split",
    )(cache)


def pick_kernel(slot_ref, split_ref, out_ref):
    for j in range(out_ref.shape[0]):
        out_ref[j] = split_ref[jnp.maximum(slot_ref[j, 0, 0], 0)]


def pick(slots, blocks):
    return pl.pallas_call(
        pick_kernel,
        out_shape=jax.ShapeDtypeStruct((slots.shape[0],) + blocks.shape[1:], bf16),
        in_specs=[SMEM, VMEM],
        out_specs=VMEM,
        compiler_params=small(4),
        name="pick",
    )(slots, blocks)


def load_memory(table_ref, arrived_ref, key_ref, value_ref, r, list_len, part):
    for i in range(list_len):
        o = table_ref[r * list_len + i]
        key_ref[i * part : (i + 1) * part, :] = arrived_ref[o, :part, :]
        value_ref[i * part : (i + 1) * part, :] = arrived_ref[o, part:, :]


def stat_row(table_ref, requests, step, r, t, rows, tiles, sections):
    section = lax.rem(table_ref[requests] + step, sections)
    return (section * rows + r) * tiles + t


def stats_kernel(list_len, part, scale2, rows, tiles, steps, table_ref, arrived_ref, *refs):
    sections = len(steps)
    q_refs, t_refs = refs[:sections], refs[sections : 2 * sections]
    stats_ref, key_ref, value_ref = refs[2 * sections :]
    r, t = pl.program_id(0), pl.program_id(1)
    total = sections * rows * tiles

    @pl.when(t == 0)
    def _():
        load_memory(table_ref, arrived_ref, key_ref, value_ref, r, list_len, part)

    for step, q_ref, t_ref in zip(steps, q_refs, t_refs):
        s = dot(key_ref[...], q_ref[0], NT)
        dp = dot(value_ref[...], t_ref[0], NT)
        raw = jnp.max(s, axis=0, keepdims=True)
        p = jnp.exp2((s - raw) * scale2)
        top = raw * scale2
        index = stat_row(table_ref, rows * list_len, step, r, t, rows, tiles, sections)
        mine = (top, jnp.sum(p, axis=0, keepdims=True), jnp.sum(p * dp, axis=0, keepdims=True))
        for kind, value in enumerate(mine):
            for c in range(sections):
                stats_ref[c, pl.ds(kind * total + index, 1), :] = value


def grad_kernel(list_len, part, scale, scale2, rows, tiles, steps, table_ref, arrived_ref, stats_ref, *refs):
    sections = len(steps)
    q_refs, t_refs = refs[:sections], refs[sections : 2 * sections]
    parcel_ref, total_ref, key_ref, value_ref, dk_ref, dv_ref = refs[2 * sections :]
    r, t = pl.program_id(0), pl.program_id(1)
    total = sections * rows * tiles

    @pl.when((r == 0) & (t == 0))
    def _():
        parcel_ref[...] = jnp.zeros_like(parcel_ref)
        tops = [stats_ref[c, :total, :] for c in range(sections)]
        top = functools.reduce(jnp.maximum, tops)
        shares = [jnp.exp2(x - top) for x in tops]
        norm = sum(a * stats_ref[c, total : 2 * total, :] for c, a in enumerate(shares))
        dots = sum(a * stats_ref[c, 2 * total :, :] for c, a in enumerate(shares))
        total_ref[:total, :] = top + jnp.log2(norm)
        total_ref[total:, :] = dots / norm

    @pl.when(t == 0)
    def _():
        load_memory(table_ref, arrived_ref, key_ref, value_ref, r, list_len, part)
        dk_ref[...] = jnp.zeros_like(dk_ref)
        dv_ref[...] = jnp.zeros_like(dv_ref)

    for step, q_ref, t_ref in zip(steps, q_refs, t_refs):
        q, tangent = q_ref[0], t_ref[0]
        index = stat_row(table_ref, rows * list_len, step, r, t, rows, tiles, sections)
        shift = total_ref[pl.ds(index, 1), :]
        delta = total_ref[pl.ds(total + index, 1), :]
        s = dot(key_ref[...], q, NT)
        dp = dot(value_ref[...], tangent, NT)
        w = jnp.exp2(s * scale2 - shift)
        w16 = w.astype(bf16)
        ds = (w * (dp - delta)).astype(bf16)
        dv_ref[...] += dot(w16, tangent, NN)
        dk_ref[...] += dot(ds, q, NN)

    @pl.when(t == tiles - 1)
    def _():
        for i in range(list_len):
            o = table_ref[r * list_len + i]
            parcel_ref[o, :part, :] = (dk_ref[i * part : (i + 1) * part, :] * scale).astype(bf16)
            parcel_ref[o, part:, :] = dv_ref[i * part : (i + 1) * part, :].astype(bf16)


def attend_kernel(list_len, part, scale2, rows, tiles, steps, table_ref, arrived_ref, total_ref, *refs):
    sections = len(steps)
    q_refs, out_refs = refs[:sections], refs[sections : 2 * sections]
    key_ref, value_ref, turned_ref = refs[2 * sections :]
    r, t = pl.program_id(0), pl.program_id(1)

    @pl.when(t == 0)
    def _():
        load_memory(table_ref, arrived_ref, key_ref, value_ref, r, list_len, part)
        turned_ref[...] = value_ref[...].astype(f32).T.astype(bf16)

    for step, q_ref, out_ref in zip(steps, q_refs, out_refs):
        index = stat_row(table_ref, rows * list_len, step, r, t, rows, tiles, sections)
        s = dot(key_ref[...], q_ref[0], NT)
        w16 = jnp.exp2(s * scale2 - total_ref[pl.ds(index, 1), :]).astype(bf16)
        out_ref[0] = dot(turned_ref[...], w16, NN).T.astype(bf16)


def plan(qs, list_len, part, width):
    rows, tokens, head_size = qs[0].shape
    scale = 1.0 / math.sqrt(head_size)
    spec = pl.BlockSpec((1, width, head_size), lambda r, t: (r, t, 0))
    pairs = rows * len(qs) * tokens * list_len * part
    return rows, tokens // width, head_size, list_len * part, scale, math.log2(math.e) * scale, spec, pairs


def cost(pairs, head_size, dots, tensors):
    return pl.CostEstimate(
        flops=2 * dots * pairs * head_size, bytes_accessed=2 * sum(x.size for x in tensors), transcendentals=pairs
    )


def row_stats(table, arrived, qs, ts, steps, list_len, part, width):
    rows, tiles, head_size, keys, _, scale2, spec, pairs = plan(qs, list_len, part, width)
    sections = len(steps)
    return pl.pallas_call(
        functools.partial(stats_kernel, list_len, part, scale2, rows, tiles, steps),
        out_shape=jax.ShapeDtypeStruct((sections, 3 * sections * rows * tiles, width), f32),
        grid=(rows, tiles),
        in_specs=[SMEM, VMEM] + [spec] * (2 * sections),
        out_specs=VMEM,
        scratch_shapes=[pltpu.VMEM((keys, head_size), bf16)] * 2,
        cost_estimate=cost(pairs, head_size, 2, qs + ts),
        name="stats",
    )(table, arrived, *qs, *ts)


def row_grads(table, arrived, stats, qs, ts, steps, list_len, part, width):
    rows, tiles, head_size, keys, scale, scale2, spec, pairs = plan(qs, list_len, part, width)
    sections = len(steps)
    return pl.pallas_call(
        functools.partial(grad_kernel, list_len, part, scale, scale2, rows, tiles, steps),
        out_shape=(
            jax.ShapeDtypeStruct(arrived.shape, bf16),
            jax.ShapeDtypeStruct((2 * sections * rows * tiles, width), f32),
        ),
        grid=(rows, tiles),
        in_specs=[SMEM, VMEM, VMEM] + [spec] * (2 * sections),
        out_specs=(VMEM, VMEM),
        scratch_shapes=[pltpu.VMEM((keys, head_size), bf16)] * 2 + [pltpu.VMEM((keys, head_size), f32)] * 2,
        cost_estimate=cost(pairs, head_size, 4, qs + ts),
        name="grads",
    )(table, arrived, stats, *qs, *ts)


def row_attend(table, arrived, totals, qs, steps, list_len, part, width):
    rows, tiles, head_size, keys, _, scale2, spec, pairs = plan(qs, list_len, part, width)
    sections = len(steps)
    return pl.pallas_call(
        functools.partial(attend_kernel, list_len, part, scale2, rows, tiles, steps),
        out_shape=[jax.ShapeDtypeStruct(qs[0].shape, bf16)] * sections,
        grid=(rows, tiles),
        in_specs=[SMEM, VMEM, VMEM] + [spec] * sections,
        out_specs=[spec] * sections,
        scratch_shapes=[pltpu.VMEM((keys, head_size), bf16)] * 2 + [pltpu.VMEM((head_size, keys), bf16)],
        cost_estimate=cost(pairs, head_size, 2, qs + qs),
        name="attend",
    )(table, arrived, totals, *qs)


def collect_kernel(slot_ref, returned_ref, grad_ref, square_ref):
    step = pl.program_id(0)
    group = returned_ref.shape[0]

    @pl.when(step == 0)
    def _():
        grad_ref[...] = jnp.zeros_like(grad_ref)

    for j in range(group):
        d = slot_ref[step * group + j, 0, 0]

        @pl.when(d >= 0)
        def _():
            grad_ref[d] = grad_ref[d] + returned_ref[j].astype(f32)

    @pl.when(step == pl.num_programs(0) - 1)
    def _():
        total = functools.reduce(jnp.add, [grad_ref[d] * grad_ref[d] for d in range(grad_ref.shape[0])])
        total = jnp.sum(total, axis=0, keepdims=True)
        for j in range(square_ref.shape[0]):
            square_ref[j] = total


def collect(slots, returned, docs):
    readers, rows, lanes = returned.shape
    group = max(1, readers // 4)
    return pl.pallas_call(
        collect_kernel,
        out_shape=(
            jax.ShapeDtypeStruct((docs, rows, lanes), f32),
            jax.ShapeDtypeStruct((readers, 1, lanes), f32),
        ),
        grid=(readers // group,),
        in_specs=[SMEM, pl.BlockSpec((group, rows, lanes), lambda i: (i, 0, 0))],
        out_specs=(VMEM, VMEM),
        compiler_params=small(8),
        name="collect",
    )(slots, returned)


def fold_kernel(square_ref, out_ref):
    total = functools.reduce(jnp.add, [square_ref[j] for j in range(square_ref.shape[0])])
    for j in range(out_ref.shape[0]):
        out_ref[j] = total


def fold(square, count):
    return pl.pallas_call(
        fold_kernel,
        out_shape=jax.ShapeDtypeStruct((count,) + square.shape[1:], f32),
        in_specs=[VMEM],
        out_specs=VMEM,
        compiler_params=small(2),
        name="fold",
    )(square)


def update_kernel(clip_limit, square_ref, grad_ref, cache_ref, momentum_ref, new_cache_ref, new_momentum_ref):
    total = functools.reduce(jnp.add, [square_ref[j] for j in range(square_ref.shape[0])])
    norm = jnp.sqrt(jnp.sum(total, axis=1, keepdims=True))
    factor = clip_limit / jnp.maximum(norm, clip_limit)
    docs, rows, _ = grad_ref.shape
    half = rows // 2

    def one(d, _):
        for kind in range(2):
            at = (d, pl.ds(kind, half, stride=2), slice(None))
            new_momentum_ref[at] = momentum_decay * momentum_ref[at] + factor * grad_ref[d, kind * half : (kind + 1) * half, :]
        new_cache_ref[d] = (cache_ref[d].astype(f32) - step_rate * new_momentum_ref[d]).astype(bf16)
        return 0

    lax.fori_loop(0, docs, one, 0)


def update(clip_limit, square, grad, cache, momentum):
    return pl.pallas_call(
        functools.partial(update_kernel, clip_limit),
        out_shape=(jax.ShapeDtypeStruct(cache.shape, bf16), jax.ShapeDtypeStruct(momentum.shape, f32)),
        in_specs=[VMEM] * 4,
        out_specs=(VMEM, VMEM),
        compiler_params=small(8),
        name="update",
    )(square, grad, cache, momentum)


def swap(x, axes):
    return lax.all_to_all(x, axes, split_axis=0, concat_axis=0, tiled=True)


def pass_on(x, ring):
    return lax.ppermute(x, "section", ring)


def body(queries, cotangent, cache, momentum, doc_lists, place):
    rows_dev, seq_len, head_count, kv_count, head_size = queries.shape
    doc_dev, len_part = cache.shape[:2]
    doc_total = place.shape[0]
    owners = doc_total // doc_dev
    list_len = doc_lists.shape[1]
    sections = lax.axis_size("section")
    tokens = seq_len * head_count

    q_own = queries.reshape(rows_dev, tokens, head_size)
    t_own = cotangent.reshape(rows_dev, tokens, head_size)
    up = [(i, (i + 1) % sections) for i in range(sections)]
    down = [(i, (i - 1) % sections) for i in range(sections)]
    across = [(i, (i + 2) % sections) for i in range(sections)]
    q_prev, t_next = pass_on(q_own, up), pass_on(t_own, down)
    q_next, t_prev = pass_on(q_own, down), pass_on(t_own, up)
    q_far, t_far = pass_on(q_prev, up), pass_on(t_next, down)
    qs, ts = (q_own, q_prev, q_next, q_far), (t_own, t_prev, t_next, t_far)
    steps = (0, 3, 1, 2)

    wanted, table = ask(doc_lists, place, owners, doc_dev)
    slots = swap(wanted, "doc")
    stored = cache.reshape(doc_dev, len_part * 2, head_size)
    outgoing = pick(slots, split(stored))
    arrived = swap(outgoing, "doc")

    width = 512
    stats = swap(row_stats(table, arrived, qs, ts, steps, list_len, len_part, width), "section")
    parcel, totals = row_grads(table, arrived, stats, qs, ts, steps, list_len, len_part, width)
    own, to_prev, to_next, to_far = row_attend(table, arrived, totals, qs, steps, list_len, len_part, width)
    shares = (own, pass_on(to_prev, down), pass_on(to_next, up), pass_on(to_far, across))
    attention = sum(x.astype(f32) for x in shares).astype(bf16).reshape(queries.shape)

    returned = swap(parcel, "doc")
    gradient, square = collect(slots, returned, doc_dev)
    planes = sections * lax.axis_size("mp")
    square = fold(swap(square, "doc"), planes)
    square = swap(square, ("section", "mp"))
    entry_count = doc_total * len_part * planes * kv_count * 2 * head_size
    clip_limit = clip_level * math.sqrt(entry_count)
    new_cache, new_momentum = update(
        clip_limit, square, gradient, stored, momentum.reshape(doc_dev, len_part * 2, head_size)
    )
    return (attention, new_cache.reshape(cache.shape), new_momentum.reshape(momentum.shape))


def solution(mesh):
    in_specs = (
        P("doc", None, "section", "mp", None),
        P("doc", None, "section", "mp", None),
        P("doc", "section", "mp", None, None),
        P("doc", "section", "mp", None, None),
        P("doc", None),
        P(),
    )
    out_specs = (
        P("doc", None, "section", "mp", None),
        P("doc", "section", "mp", None, None),
        P("doc", "section", "mp", None, None),
    )

    return jax.shard_map(body, mesh=mesh, in_specs=in_specs, out_specs=out_specs, check_vma=False)
```

time: 202 us -> 182 us (0.901)
  blocking collectives: 54.7 us -> 25.4 us
  starting transfers between devices: 45.9 us -> 67.1 us
  waiting for transfers between devices: 65.1 us -> 56.2 us
  other arithmetic: 4.24 us -> 1.07 us
    all_to_all x3 -> x2, blocking collectives: 54.7 us -> 25.4 us  [swap(): return lax.all_to_all(x, axes, split_axis=0, concat_axis=0, tiled=True)]
    all_to_all x3 -> x4, starting transfers between devices: 24.4 us -> 40.9 us  [swap(): return lax.all_to_all(x, axes, split_axis=0, concat_axis=0, tiled=True)]
    ppermute x7 -> x9, waiting for transfers between devices: 34.3 us -> 22.1 us  [pass_on(): return lax.ppermute(x, 'section', ring)]
    pallas_call x2 -> x5, Pallas kernels: 4.68 us -> 12 us  [the longest x1 7.3 us: row_attend(): pl.pallas_call(functools.partial(attend_kernel, list_len, part, scale2, r...]
    ppermute x7 -> x9, starting transfers between devices: 21.5 us -> 26.2 us  [pass_on(): return lax.ppermute(x, 'section', ring)]
    pallas_call x1, Pallas kernels: 12.4 us -> 7.98 us  [row_grads(): pl.pallas_call(functools.partial(grad_kernel, list_len, part, scale, scal...]
    all_to_all x3 -> x4, waiting for transfers between devices: 30.8 us -> 34.1 us  [swap(): return lax.all_to_all(x, axes, split_axis=0, concat_axis=0, tiled=True)]
    another operation x1 -> x0, other arithmetic: 2.29 us -> none  [body(): both = jnp.stack([q_own, t_own])]
  transfers between devices with their start and end apart: 10 -> 13, of which waited for: 4 -> 7; matrix products, arithmetic and copies ran while one was open for 2% -> 1% of each run, Pallas kernels for 3% -> 5%
where the time goes in v2:
time: 182 us; the launch traced here: 181 us
  starting transfers between devices  67.1 us (37%)
  waiting for transfers between devices  56.2 us (31%)
  Pallas kernels  28.3 us (16%)
  blocking collectives  25.4 us (14%)
    all_to_all x4, starting transfers between devices, swap(): return lax.all_to_all(x, axes, split_axis=0, concat_axis=0, tiled=True)  40.9 us
    all_to_all x4, waiting for transfers between devices, swap(): return lax.all_to_all(x, axes, split_axis=0, concat_axis=0, tiled=True)  34.1 us
    ppermute x9, starting transfers between devices, pass_on(): return lax.ppermute(x, 'section', ring)  26.2 us
    all_to_all x2, blocking collectives, swap(): return lax.all_to_all(x, axes, split_axis=0, concat_axis=0, tiled=True)  25.4 us
    ppermute x9, waiting for transfers between devices, pass_on(): return lax.ppermute(x, 'section', ring)  22.1 us
    pallas_call x1, Pallas kernels, row_grads(): pl.pallas_call(functools.partial(grad_kernel, list_len, part, scale, scal...  7.98 us
    pallas_call x1, Pallas kernels, row_attend(): pl.pallas_call(functools.partial(attend_kernel, list_len, part, scale2, r...  7.3 us
    pallas_call x1, Pallas kernels, row_stats(): pl.pallas_call(functools.partial(stats_kernel, list_len, part, scale2, ro...  6.48 us
  transfers between devices with their start and end apart: 13, of which 7 were waited for; matrix products, arithmetic and copies ran while one was open for 1% of the time, Pallas kernels for 5%

profile of v2, /device:TPU:1, one launch (start us, length us, event | category | flops | bytes accessed | tf_op | source)
XLA Modules:
  0.0 180.8 jit_solution(12369350395552485856)
XLA Ops:
  2.2 16.7 %all-to-all-start = ((s32[32,1,1]{2,1,0:T(1,128)}), s32[32,1,1]{2,1,0:T(1,128)S(1)}, u32[]{:S(2)}, u32[]{:S(2)}) async-start(s32[32,1,1]{2,1,0:T(1,128)} %get-tuple-element.16), calls=%async_computation | async-start | bytes 32768 | tf_op jit(solution)/shard_map/all_to_all | solution.py:344
  20.1 10.6 %all-to-all-done.slot_ref = s32[32,1,1]{2,1,0:T(1,128)S(1)} async-done(((s32[32,1,1]{2,1,0:T(1,128)}), s32[32,1,1]{2,1,0:T(1,128)S(1)}, u32[]{:S(2)}, u32[]{:S(2)}) %all-to-all-start) | async-done | bytes 160 | tf_op jit(solution)/shard_map/all_to_all | solution.py:344
  32.4 4.6 %all-to-all-start.1 = ((bf16[32,64,128]{2,1,0:T(8,128)(2,1)}), bf16[32,64,128]{2,1,0:T(8,128)(2,1)S(1)}, u32[]{:S(2)}, u32[]{:S(2)}) async-start(bf16[32,64,128]{2,1,0:T(8,128)(2,1)} %pick.1), calls=%async_computation.1 | async-start | bytes 1048576 | tf_op jit(solution)/shard_map/all_to_all | solution.py:344
  37.0 3.1 %collective-permute-start = (bf16[2,1024,128]{2,1,0:T(8,128)(2,1)S(1)}, bf16[2,1024,128]{2,1,0:T(8,128)(2,1)S(1)}, u32[]{:S(2)}, u32[]{:S(2)}) collective-permute-start(bf16[2,1024,128]{2,1,0:T(8,128)(2,1)S(1)} %bitcast.24), channel_id=1, source_target_pairs={{0,128},{128,256},{256,384},{384,0},{1,129},{129,257},{257,385},{3... | collective-permute-start | bytes 1572872 | tf_op jit(solution)/shard_map/ppermute | solution.py:348
  40.1 3.4 %collective-permute-start.4 = (bf16[2,1024,128]{2,1,0:T(8,128)(2,1)S(1)}, bf16[2,1024,128]{2,1,0:T(8,128)(2,1)S(1)}, u32[]{:S(2)}, u32[]{:S(2)}) collective-permute-start(bf16[2,1024,128]{2,1,0:T(8,128)(2,1)S(1)} %bitcast.19), channel_id=1, source_target_pairs={{0,384},{128,0},{256,128},{384,256},{1,385},{129,1},{257,129},{385... | collective-permute-start | bytes 1572872 | tf_op jit(solution)/shard_map/ppermute | solution.py:348
  43.5 3.2 %collective-permute-start.1 = (bf16[2,1024,128]{2,1,0:T(8,128)(2,1)S(1)}, bf16[2,1024,128]{2,1,0:T(8,128)(2,1)S(1)}, u32[]{:S(2)}, u32[]{:S(2)}) collective-permute-start(bf16[2,1024,128]{2,1,0:T(8,128)(2,1)S(1)} %bitcast.25), channel_id=1, source_target_pairs={{0,384},{128,0},{256,128},{384,256},{1,385},{129,1},{257,129},{385... | collective-permute-start | bytes 1572872 | tf_op jit(solution)/shard_map/ppermute | solution.py:348
  46.7 2.1 %collective-permute-start.3 = (bf16[2,1024,128]{2,1,0:T(8,128)(2,1)S(1)}, bf16[2,1024,128]{2,1,0:T(8,128)(2,1)S(1)}, u32[]{:S(2)}, u32[]{:S(2)}) collective-permute-start(bf16[2,1024,128]{2,1,0:T(8,128)(2,1)S(1)} %bitcast.20), channel_id=1, source_target_pairs={{0,128},{128,256},{256,384},{384,0},{1,129},{129,257},{257,385},{3... | collective-permute-start | bytes 1572872 | tf_op jit(solution)/shard_map/ppermute | solution.py:348
  48.8 4.4 %collective-permute-done.refs_1_ = bf16[2,1024,128]{2,1,0:T(8,128)(2,1)S(1)} collective-permute-done((bf16[2,1024,128]{2,1,0:T(8,128)(2,1)S(1)}, bf16[2,1024,128]{2,1,0:T(8,128)(2,1)S(1)}, u32[]{:S(2)}, u32[]{:S(2)}) %collective-permute-start) | collective-permute-done | bytes 524320 | tf_op jit(solution)/shard_map/ppermute | solution.py:348
  53.2 1.9 %collective-permute-start.2 = (bf16[2,1024,128]{2,1,0:T(8,128)(2,1)S(1)}, bf16[2,1024,128]{2,1,0:T(8,128)(2,1)S(1)}, u32[]{:S(2)}, u32[]{:S(2)}) collective-permute-start(bf16[2,1024,128]{2,1,0:T(8,128)(2,1)S(1)} %collective-permute-done.refs_1_), channel_id=1, source_target_pairs={{0,128},{128,256},{256,384},{384,0},{1,129},{129,257},{257,385},{3... | collective-permute-start | bytes 1572872 | tf_op jit(solution)/shard_map/ppermute | solution.py:348
  55.1 4.6 %collective-permute-start.5 = (bf16[2,1024,128]{2,1,0:T(8,128)(2,1)S(1)}, bf16[2,1024,128]{2,1,0:T(8,128)(2,1)}, u32[]{:S(2)}, u32[]{:S(2)}) collective-permute-start(bf16[2,1024,128]{2,1,0:T(8,128)(2,1)S(1)} %collective-permute-done.4.refs_6_), channel_id=1, source_target_pairs={{0,384},{128,0},{256,128},{384,256},{1,385},{129,1},{257,129},{385... | collective-permute-start | bytes 1572872 | tf_op jit(solution)/shard_map/ppermute | solution.py:348
  59.7 6.4 %collective-permute-done.1.refs_2_ = bf16[2,1024,128]{2,1,0:T(8,128)(2,1)S(1)} collective-permute-done((bf16[2,1024,128]{2,1,0:T(8,128)(2,1)S(1)}, bf16[2,1024,128]{2,1,0:T(8,128)(2,1)S(1)}, u32[]{:S(2)}, u32[]{:S(2)}) %collective-permute-start.1) | collective-permute-done | bytes 524320 | tf_op jit(solution)/shard_map/ppermute | solution.py:348
  66.1 9.6 %collective-permute-done.2.refs_3_ = bf16[2,1024,128]{2,1,0:T(8,128)(2,1)S(1)} collective-permute-done((bf16[2,1024,128]{2,1,0:T(8,128)(2,1)S(1)}, bf16[2,1024,128]{2,1,0:T(8,128)(2,1)S(1)}, u32[]{:S(2)}, u32[]{:S(2)}) %collective-permute-start.2) | collective-permute-done | bytes 524320 | tf_op jit(solution)/shard_map/ppermute | solution.py:348
  78.2 6.5 %stats.1 = f32[4,48,512]{2,1,0:T(8,128)} custom-call(s32[17]{0:T(128)} %get-tuple-element.15.table_ref, bf16[32,64,128]{2,1,0:T(8,128)(2,1)} %copy-done.3, bf16[2,1024,128]{2,1,0:T(8,128)(2,1)} %bitcast.21, bf16[2,1024,128]{2,1,0:T(8,128)(2,1)} %copy-done.7, bf16[2,1024,128]{2,1,0:T(8,128)(2,1)} %copy-done.8, bf16[2,1024,128]{2,1,0:T(8,128)(2,1)} %copy-done.9, ...), custom_call_target="tpu_custom_call" | custom-call | flops 1073741824 | bytes 4194304 | tf_op jit(solution)/shard_map/stats/pallas_call | solution.py:213
  84.7 10.4 %all_to_all.30.stats_ref = f32[4,48,512]{2,1,0:T(8,128)} all-to-all(f32[4,48,512]{2,1,0:T(8,128)} %stats.1), channel_id=1, replica_groups=mesh['section'=4,'doc'=32,'mp'=4] {'section'}, dimensions={0} | all-to-all | bytes 786432 | tf_op jit(solution)/shard_map/all_to_all | solution.py:344
  95.1 8.0 %grads.1 = (bf16[32,64,128]{2,1,0:T(8,128)(2,1)}, f32[32,512]{1,0:T(8,128)}) custom-call(s32[17]{0:T(128)} %get-tuple-element.15.table_ref, bf16[32,64,128]{2,1,0:T(8,128)(2,1)} %copy-done.3, f32[4,48,512]{2,1,0:T(8,128)} %all_to_all.30.stats_ref, bf16[2,1024,128]{2,1,0:T(8,128)(2,1)} %bitcast.22, bf16[2,1024,128]{2,1,0:T(8,128)(2,1)} %copy-done.7, ...), custom_call_target="tpu_custom_call" | custom-call | flops 2147483648 | bytes 4194304 | tf_op jit(solution)/shard_map/grads/pallas_call | solution.py:228
  103.1 14.7 %all-to-all-start.3 = ((bf16[32,64,128]{2,1,0:T(8,128)(2,1)}), bf16[32,64,128]{2,1,0:T(8,128)(2,1)S(1)}, u32[]{:S(2)}, u32[]{:S(2)}) async-start(bf16[32,64,128]{2,1,0:T(8,128)(2,1)} %get-tuple-element.22), calls=%async_computation.3 | async-start | bytes 1048576 | tf_op jit(solution)/shard_map/all_to_all | solution.py:344
  117.8 7.3 %attend.1 = (bf16[2,1024,128]{2,1,0:T(8,128)(2,1)}, bf16[2,1024,128]{2,1,0:T(8,128)(2,1)}, bf16[2,1024,128]{2,1,0:T(8,128)(2,1)}, bf16[2,1024,128]{2,1,0:T(8,128)(2,1)}) custom-call(s32[17]{0:T(128)} %get-tuple-element.15.table_ref, bf16[32,64,128]{2,1,0:T(8,128)(2,1)} %copy-done.3, f32[32,512]{1,0:T(8,128)} %get-tuple-element.17.total_ref, ...), custom_call_target="tpu_custom_call" | custom-call | flops 1073741824 | bytes 4194304 | tf_op jit(solution)/shard_map/attend/pallas_call | solution.py:246
  125.1 2.9 %collective-permute-start.6 = (bf16[2,1024,128]{2,1,0:T(8,128)(2,1)}, bf16[2,1024,128]{2,1,0:T(8,128)(2,1)S(1)}, u32[]{:S(2)}, u32[]{:S(2)}) collective-permute-start(bf16[2,1024,128]{2,1,0:T(8,128)(2,1)} %get-tuple-element.19), channel_id=1, source_target_pairs={{0,384},{128,0},{256,128},{384,256},{1,385},{129,1},{257,129},{385... | collective-permute-start | bytes 1572872 | tf_op jit(solution)/shard_map/ppermute | solution.py:348
  128.0 2.5 %collective-permute-start.7 = (bf16[2,1024,128]{2,1,0:T(8,128)(2,1)}, bf16[2,1024,128]{2,1,0:T(8,128)(2,1)S(1)}, u32[]{:S(2)}, u32[]{:S(2)}) collective-permute-start(bf16[2,1024,128]{2,1,0:T(8,128)(2,1)} %get-tuple-element.20), channel_id=1, source_target_pairs={{0,128},{128,256},{256,384},{384,0},{1,129},{129,257},{257,385},{3... | collective-permute-start | bytes 1572872 | tf_op jit(solution)/shard_map/ppermute | solution.py:348
  130.5 2.5 %collective-permute-start.8 = (bf16[2,1024,128]{2,1,0:T(8,128)(2,1)}, bf16[2,1024,128]{2,1,0:T(8,128)(2,1)S(1)}, u32[]{:S(2)}, u32[]{:S(2)}) collective-permute-start(bf16[2,1024,128]{2,1,0:T(8,128)(2,1)} %get-tuple-element.21), channel_id=1, source_target_pairs={{0,256},{128,384},{256,0},{384,128},{1,257},{129,385},{257,1},{385... | collective-permute-start | bytes 1572872 | tf_op jit(solution)/shard_map/ppermute | solution.py:348
  133.1 18.3 %all-to-all-done.3.returned_ref = bf16[32,64,128]{2,1,0:T(8,128)(2,1)S(1)} async-done(((bf16[32,64,128]{2,1,0:T(8,128)(2,1)}), bf16[32,64,128]{2,1,0:T(8,128)(2,1)S(1)}, u32[]{:S(2)}, u32[]{:S(2)}) %all-to-all-start.3) | async-done | bytes 524320 | tf_op jit(solution)/shard_map/all_to_all | solution.py:344
  152.6 15.0 %all_to_all.31.square_ref = f32[32,1,128]{2,1,0:T(1,128)S(1)} all-to-all(f32[32,1,128]{2,1,0:T(1,128)S(1)} %get-tuple-element.23), channel_id=1, replica_groups=mesh['section'=4,'doc'=32,'mp'=4] {'doc'}, dimensions={0} | all-to-all | bytes 32768 | tf_op jit(solution)/shard_map/all_to_all | solution.py:344
  168.3 4.9 %all-to-all-start.5 = ((f32[16,1,128]{2,1,0:T(1,128)}), f32[16,1,128]{2,1,0:T(1,128)S(1)}, u32[]{:S(2)}, u32[]{:S(2)}) async-start(f32[16,1,128]{2,1,0:T(1,128)} %fold.1), calls=%async_computation.5 | async-start | bytes 16384 | tf_op jit(solution)/shard_map/all_to_all | solution.py:344
  174.3 5.2 %all-to-all-done.5.square_ref = f32[16,1,128]{2,1,0:T(1,128)S(1)} async-done(((f32[16,1,128]{2,1,0:T(1,128)}), f32[16,1,128]{2,1,0:T(1,128)S(1)}, u32[]{:S(2)}, u32[]{:S(2)}) %all-to-all-start.5) | async-done | bytes 8224 | tf_op jit(solution)/shard_map/all_to_all | solution.py:344
  (38 shorter events, 11.2 us)
Async XLA Ops:
  2.2 28.5 %all-to-all-start = ((s32[32,1,1]{2,1,0:T(1,128)}), s32[32,1,1]{2,1,0:T(1,128)S(1)}, u32[]{:S(2)}, u32[]{:S(2)}) async-start(s32[32,1,1]{2,1,0:T(1,128)} %get-tuple-element.16), calls=%async_computation | async-start | bytes 32768 | tf_op jit(solution)/shard_map/all_to_all | solution.py:344
  19.0 1.0 copy-start
  32.4 4.6 %copy-start.6 = (bf16[2,512,2,1,128]{4,2,3,1,0:T(2,128)(2,1)S(1)}, bf16[2,512,2,1,128]{4,2,3,1,0:T(2,128)(2,1)}, u32[]{:S(2)}) copy-start(bf16[2,512,2,1,128]{4,2,3,1,0:T(2,128)(2,1)} %param.6) | copy-start | bytes 1572868
  32.4 7.7 %copy-start.5 = (bf16[2,512,2,1,128]{4,2,3,1,0:T(2,128)(2,1)S(1)}, bf16[2,512,2,1,128]{4,2,3,1,0:T(2,128)(2,1)}, u32[]{:S(2)}) copy-start(bf16[2,512,2,1,128]{4,2,3,1,0:T(2,128)(2,1)} %param.7) | copy-start | bytes 1572868
  32.4 45.1 %all-to-all-start.1 = ((bf16[32,64,128]{2,1,0:T(8,128)(2,1)}), bf16[32,64,128]{2,1,0:T(8,128)(2,1)S(1)}, u32[]{:S(2)}, u32[]{:S(2)}) async-start(bf16[32,64,128]{2,1,0:T(8,128)(2,1)} %pick.1), calls=%async_computation.1 | async-start | bytes 1048576 | tf_op jit(solution)/shard_map/all_to_all | solution.py:344
  37.0 16.2 %collective-permute-start = (bf16[2,1024,128]{2,1,0:T(8,128)(2,1)S(1)}, bf16[2,1024,128]{2,1,0:T(8,128)(2,1)S(1)}, u32[]{:S(2)}, u32[]{:S(2)}) collective-permute-start(bf16[2,1024,128]{2,1,0:T(8,128)(2,1)S(1)} %bitcast.24), channel_id=1, source_target_pairs={{0,128},{128,256},{256,384},{384,0},{1,129},{129,257},{257,385},{3... | collective-permute-start | bytes 1572872 | tf_op jit(solution)/shard_map/ppermute | solution.py:348
  40.1 15.0 %collective-permute-start.4 = (bf16[2,1024,128]{2,1,0:T(8,128)(2,1)S(1)}, bf16[2,1024,128]{2,1,0:T(8,128)(2,1)S(1)}, u32[]{:S(2)}, u32[]{:S(2)}) collective-permute-start(bf16[2,1024,128]{2,1,0:T(8,128)(2,1)S(1)} %bitcast.19), channel_id=1, source_target_pairs={{0,384},{128,0},{256,128},{384,256},{1,385},{129,1},{257,129},{385... | collective-permute-start | bytes 1572872 | tf_op jit(solution)/shard_map/ppermute | solution.py:348
  43.5 22.6 %collective-permute-start.1 = (bf16[2,1024,128]{2,1,0:T(8,128)(2,1)S(1)}, bf16[2,1024,128]{2,1,0:T(8,128)(2,1)S(1)}, u32[]{:S(2)}, u32[]{:S(2)}) collective-permute-start(bf16[2,1024,128]{2,1,0:T(8,128)(2,1)S(1)} %bitcast.25), channel_id=1, source_target_pairs={{0,384},{128,0},{256,128},{384,256},{1,385},{129,1},{257,129},{385... | collective-permute-start | bytes 1572872 | tf_op jit(solution)/shard_map/ppermute | solution.py:348
  46.7 19.4 %collective-permute-start.3 = (bf16[2,1024,128]{2,1,0:T(8,128)(2,1)S(1)}, bf16[2,1024,128]{2,1,0:T(8,128)(2,1)S(1)}, u32[]{:S(2)}, u32[]{:S(2)}) collective-permute-start(bf16[2,1024,128]{2,1,0:T(8,128)(2,1)S(1)} %bitcast.20), channel_id=1, source_target_pairs={{0,128},{128,256},{256,384},{384,0},{1,129},{129,257},{257,385},{3... | collective-permute-start | bytes 1572872 | tf_op jit(solution)/shard_map/ppermute | solution.py:348
  53.2 24.2 %copy-start.7 = (bf16[2,1024,128]{2,1,0:T(8,128)(2,1)}, bf16[2,1024,128]{2,1,0:T(8,128)(2,1)S(1)}, u32[]{:S(2)}) copy-start(bf16[2,1024,128]{2,1,0:T(8,128)(2,1)S(1)} %collective-permute-done.refs_1_) | copy-start | bytes 1572868
  53.2 22.5 %collective-permute-start.2 = (bf16[2,1024,128]{2,1,0:T(8,128)(2,1)S(1)}, bf16[2,1024,128]{2,1,0:T(8,128)(2,1)S(1)}, u32[]{:S(2)}, u32[]{:S(2)}) collective-permute-start(bf16[2,1024,128]{2,1,0:T(8,128)(2,1)S(1)} %collective-permute-done.refs_1_), channel_id=1, source_target_pairs={{0,128},{128,256},{256,384},{384,0},{1,129},{129,257},{257,385},{3... | collective-permute-start | bytes 1572872 | tf_op jit(solution)/shard_map/ppermute | solution.py:348
  55.1 20.5 %copy-start.10 = (bf16[2,1024,128]{2,1,0:T(8,128)(2,1)}, bf16[2,1024,128]{2,1,0:T(8,128)(2,1)S(1)}, u32[]{:S(2)}) copy-start(bf16[2,1024,128]{2,1,0:T(8,128)(2,1)S(1)} %collective-permute-done.4.refs_6_) | copy-start | bytes 1572868
  55.1 22.3 %collective-permute-start.5 = (bf16[2,1024,128]{2,1,0:T(8,128)(2,1)S(1)}, bf16[2,1024,128]{2,1,0:T(8,128)(2,1)}, u32[]{:S(2)}, u32[]{:S(2)}) collective-permute-start(bf16[2,1024,128]{2,1,0:T(8,128)(2,1)S(1)} %collective-permute-done.4.refs_6_), channel_id=1, source_target_pairs={{0,384},{128,0},{256,128},{384,256},{1,385},{129,1},{257,129},{385... | collective-permute-start | bytes 1572872 | tf_op jit(solution)/shard_map/ppermute | solution.py:348
  66.1 11.4 %copy-start.8 = (bf16[2,1024,128]{2,1,0:T(8,128)(2,1)}, bf16[2,1024,128]{2,1,0:T(8,128)(2,1)S(1)}, u32[]{:S(2)}) copy-start(bf16[2,1024,128]{2,1,0:T(8,128)(2,1)S(1)} %collective-permute-done.1.refs_2_) | copy-start | bytes 1572868
  66.1 9.6 %copy-start.11 = (bf16[2,1024,128]{2,1,0:T(8,128)(2,1)}, bf16[2,1024,128]{2,1,0:T(8,128)(2,1)S(1)}, u32[]{:S(2)}) copy-start(bf16[2,1024,128]{2,1,0:T(8,128)(2,1)S(1)} %collective-permute-done.3.refs_5_) | copy-start | bytes 1572868
  75.7 1.8 copy-start.9
  103.1 48.2 %all-to-all-start.3 = ((bf16[32,64,128]{2,1,0:T(8,128)(2,1)}), bf16[32,64,128]{2,1,0:T(8,128)(2,1)S(1)}, u32[]{:S(2)}, u32[]{:S(2)}) async-start(bf16[32,64,128]{2,1,0:T(8,128)(2,1)} %get-tuple-element.22), calls=%async_computation.3 | async-start | bytes 1048576 | tf_op jit(solution)/shard_map/all_to_all | solution.py:344
  125.1 48.1 %copy-start.4 = (bf16[2,1024,128]{2,1,0:T(8,128)(2,1)S(1)}, bf16[2,1024,128]{2,1,0:T(8,128)(2,1)}, u32[]{:S(2)}) copy-start(bf16[2,1024,128]{2,1,0:T(8,128)(2,1)} %get-tuple-element.18) | copy-start | bytes 1572868
  125.1 48.1 %collective-permute-start.6 = (bf16[2,1024,128]{2,1,0:T(8,128)(2,1)}, bf16[2,1024,128]{2,1,0:T(8,128)(2,1)S(1)}, u32[]{:S(2)}, u32[]{:S(2)}) collective-permute-start(bf16[2,1024,128]{2,1,0:T(8,128)(2,1)} %get-tuple-element.19), channel_id=1, source_target_pairs={{0,384},{128,0},{256,128},{384,256},{1,385},{129,1},{257,129},{385... | collective-permute-start | bytes 1572872 | tf_op jit(solution)/shard_map/ppermute | solution.py:348
  128.0 45.2 %collective-permute-start.7 = (bf16[2,1024,128]{2,1,0:T(8,128)(2,1)}, bf16[2,1024,128]{2,1,0:T(8,128)(2,1)S(1)}, u32[]{:S(2)}, u32[]{:S(2)}) collective-permute-start(bf16[2,1024,128]{2,1,0:T(8,128)(2,1)} %get-tuple-element.20), channel_id=1, source_target_pairs={{0,128},{128,256},{256,384},{384,0},{1,129},{129,257},{257,385},{3... | collective-permute-start | bytes 1572872 | tf_op jit(solution)/shard_map/ppermute | solution.py:348
  130.5 42.7 %collective-permute-start.8 = (bf16[2,1024,128]{2,1,0:T(8,128)(2,1)}, bf16[2,1024,128]{2,1,0:T(8,128)(2,1)S(1)}, u32[]{:S(2)}, u32[]{:S(2)}) collective-permute-start(bf16[2,1024,128]{2,1,0:T(8,128)(2,1)} %get-tuple-element.21), channel_id=1, source_target_pairs={{0,256},{128,384},{256,0},{384,128},{1,257},{129,385},{257,1},{385... | collective-permute-start | bytes 1572872 | tf_op jit(solution)/shard_map/ppermute | solution.py:348
  168.3 11.3 %all-to-all-start.5 = ((f32[16,1,128]{2,1,0:T(1,128)}), f32[16,1,128]{2,1,0:T(1,128)S(1)}, u32[]{:S(2)}, u32[]{:S(2)}) async-start(f32[16,1,128]{2,1,0:T(1,128)} %fold.1), calls=%async_computation.5 | async-start | bytes 16384 | tf_op jit(solution)/shard_map/all_to_all | solution.py:344
  173.2 6.3 %copy-start.1 = (bf16[16,32,1,2,128]{4,3,2,1,0:T(2,128)(2,1)S(1)}, bf16[16,32,1,2,128]{4,3,2,1,0:T(2,128)(2,1)}, u32[]{:S(2)}) copy-start(bf16[16,32,1,2,128]{4,3,2,1,0:T(2,128)(2,1)} %param.8) | copy-start | bytes 786436
  173.2 6.3 %copy-start.2 = (f32[16,32,1,2,128]{4,3,2,1,0:T(2,128)S(1)}, f32[16,32,1,2,128]{4,3,2,1,0:T(2,128)}, u32[]{:S(2)}) copy-start(f32[16,32,1,2,128]{4,3,2,1,0:T(2,128)} %param.9) | copy-start | bytes 1572868
  (1 other events, 0.8 us)

commit v3 on v2

--- a/solution.py
+++ b/solution.py
@@ -106,28 +106,64 @@
     return (section * rows + r) * tiles + t
 
 
-def stats_kernel(list_len, part, scale2, rows, tiles, steps, table_ref, arrived_ref, *refs):
-    sections = len(steps)
-    q_refs, t_refs = refs[:sections], refs[sections : 2 * sections]
-    stats_ref, key_ref, value_ref = refs[2 * sections :]
-    r, t = pl.program_id(0), pl.program_id(1)
+def tile_stats(all_ref, table_ref, key_ref, value_ref, q, t, scale2, step, r, n, rows, tiles, sections, requests):
     total = sections * rows * tiles
-
-    @pl.when(t == 0)
-    def _():
-        load_memory(table_ref, arrived_ref, key_ref, value_ref, r, list_len, part)
-
+    s = dot(key_ref[...], q, NT)
+    dp = dot(value_ref[...], t, NT)
+    raw = jnp.max(s, axis=0, keepdims=True)
+    p = jnp.exp2((s - raw) * scale2)
+    index = stat_row(table_ref, requests, step, r, n, rows, tiles, sections)
+    all_ref[pl.ds(index, 1), :] = raw * scale2
+    all_ref[pl.ds(total + index, 1), :] = jnp.sum(p, axis=0, keepdims=True)
+    all_ref[pl.ds(2 * total + index, 1), :] = jnp.sum(p * dp, axis=0, keepdims=True)
+
+
+def stats_kernel(list_len, part, scale2, rows, width, sections, steps, table_ref, arrived_ref, *refs):
+    count = len(steps)
+    q_refs, t_refs = refs[:count], refs[count : 2 * count]
+    all_ref, key_ref, value_ref = refs[2 * count :]
+    r = pl.program_id(0)
+    tiles = q_refs[0].shape[1] // width
+    load_memory(table_ref, arrived_ref, key_ref, value_ref, r, list_len, part)
     for step, q_ref, t_ref in zip(steps, q_refs, t_refs):
-        s = dot(key_ref[...], q_ref[0], NT)
-        dp = dot(value_ref[...], t_ref[0], NT)
-        raw = jnp.max(s, axis=0, keepdims=True)
-        p = jnp.exp2((s - raw) * scale2)
-        top = raw * scale2
-        index = stat_row(table_ref, rows * list_len, step, r, t, rows, tiles, sections)
-        mine = (top, jnp.sum(p, axis=0, keepdims=True), jnp.sum(p * dp, axis=0, keepdims=True))
-        for kind, value in enumerate(mine):
-            for c in range(sections):
-                stats_ref[c, pl.ds(kind * total + index, 1), :] = value
+        for n in range(tiles):
+            at = slice(n * width, (n + 1) * width)
+            tile_stats(
+                all_ref, table_ref, key_ref, value_ref, q_ref[0, at, :], t_ref[0, at, :],
+                scale2, step, r, n, rows, tiles, sections, rows * list_len,
+            )
+
+
+def far_kernel(
+    list_len, part, scale2, width, sections, step, table_ref, arrived_ref, near_ref, q_hbm, t_hbm,
+    stats_ref, all_ref, key_ref, value_ref, q_ref, t_ref, sem,
+):
+    rows = q_hbm.shape[0]
+    tiles = q_hbm.shape[1] // width
+    copies = [
+        [
+            pltpu.make_async_copy(x.at[r], y.at[r], sem.at[r, n])
+            for n, (x, y) in enumerate(((q_hbm, q_ref), (t_hbm, t_ref)))
+        ]
+        for r in range(rows)
+    ]
+    for pair in copies:
+        for copy in pair:
+            copy.start()
+    all_ref[...] = near_ref[...]
+    for r in range(rows):
+        load_memory(table_ref, arrived_ref, key_ref.at[r], value_ref.at[r], r, list_len, part)
+    for r in range(rows):
+        for copy in copies[r]:
+            copy.wait()
+        for n in range(tiles):
+            at = slice(n * width, (n + 1) * width)
+            tile_stats(
+                all_ref, table_ref, key_ref.at[r], value_ref.at[r], q_ref[r, at, :], t_ref[r, at, :],
+                scale2, step, r, n, rows, tiles, sections, rows * list_len,
+            )
+    for c in range(sections):
+        stats_ref[c] = all_ref[...]
 
 
 def grad_kernel(list_len, part, scale, scale2, rows, tiles, steps, table_ref, arrived_ref, stats_ref, *refs):
@@ -207,19 +243,36 @@
     )
 
 
-def row_stats(table, arrived, qs, ts, steps, list_len, part, width):
-    rows, tiles, head_size, keys, _, scale2, spec, pairs = plan(qs, list_len, part, width)
-    sections = len(steps)
-    return pl.pallas_call(
-        functools.partial(stats_kernel, list_len, part, scale2, rows, tiles, steps),
-        out_shape=jax.ShapeDtypeStruct((sections, 3 * sections * rows * tiles, width), f32),
-        grid=(rows, tiles),
-        in_specs=[SMEM, VMEM] + [spec] * (2 * sections),
+def row_stats(table, arrived, qs, ts, steps, sections, list_len, part, width):
+    rows, tiles, head_size, keys, _, scale2, _, pairs = plan(qs, list_len, part, width)
+    spec = pl.BlockSpec((1, tiles * width, head_size), lambda r: (r, 0, 0))
+    return pl.pallas_call(
+        functools.partial(stats_kernel, list_len, part, scale2, rows, width, sections, steps),
+        out_shape=jax.ShapeDtypeStruct((3 * sections * rows * tiles, width), f32),
+        grid=(rows,),
+        in_specs=[SMEM, VMEM] + [spec] * (2 * len(steps)),
         out_specs=VMEM,
         scratch_shapes=[pltpu.VMEM((keys, head_size), bf16)] * 2,
         cost_estimate=cost(pairs, head_size, 2, qs + ts),
         name="stats",
     )(table, arrived, *qs, *ts)
+
+
+def far_stats(table, arrived, near, q, t, step, sections, list_len, part, width):
+    rows, _, head_size, keys, _, scale2, _, pairs = plan((q,), list_len, part, width)
+    return pl.pallas_call(
+        functools.partial(far_kernel, list_len, part, scale2, width, sections, step),
+        out_shape=jax.ShapeDtypeStruct((sections,) + near.shape, f32),
+        in_specs=[SMEM, VMEM, VMEM] + [pl.BlockSpec(memory_space=pl.ANY)] * 2,
+        out_specs=VMEM,
+        scratch_shapes=[pltpu.VMEM(near.shape, f32)]
+        + [pltpu.VMEM((rows, keys, head_size), bf16)] * 2
+        + [pltpu.VMEM(q.shape, bf16)] * 2
+        + [pltpu.SemaphoreType.DMA((rows, 2))],
+        cost_estimate=cost(pairs, head_size, 2, (q, t)),
+        compiler_params=pltpu.CompilerParams(vmem_limit_bytes=67043328),
+        name="far",
+    )(table, arrived, near, q, t)
 
 
 def row_grads(table, arrived, stats, qs, ts, steps, list_len, part, width):
@@ -375,7 +428,9 @@
     arrived = swap(outgoing, "doc")
 
     width = 512
-    stats = swap(row_stats(table, arrived, qs, ts, steps, list_len, len_part, width), "section")
+    near = row_stats(table, arrived, qs[:3], ts[:3], steps[:3], sections, list_len, len_part, width)
+    stats = far_stats(table, arrived, near, qs[3], ts[3], steps[3], sections, list_len, len_part, width)
+    stats = swap(stats, "section")
     parcel, totals = row_grads(table, arrived, stats, qs, ts, steps, list_len, len_part, width)
     own, to_prev, to_next, to_far = row_attend(table, arrived, totals, qs, steps, list_len, len_part, width)
     shares = (own, pass_on(to_prev, down), pass_on(to_next, up), pass_on(to_far, across))

time: 182 us -> 178 us (0.978)
  waiting for transfers between devices: 56.2 us -> 50.4 us
  Pallas kernels: 28.3 us -> 30.7 us
    ppermute x9, waiting for transfers between devices: 22.1 us -> 12.1 us  [pass_on(): return lax.ppermute(x, 'section', ring)]
    all_to_all x4, waiting for transfers between devices: 34.1 us -> 38.3 us  [swap(): return lax.all_to_all(x, axes, split_axis=0, concat_axis=0, tiled=True)]
    pallas_call x0 -> x1, Pallas kernels: none -> 3.92 us  [far_stats(): pl.pallas_call(functools.partial(far_kernel, list_len, part, scale2, widt...]
  transfers between devices with their start and end apart: 13 -> 13, of which waited for: 7 -> 7; matrix products, arithmetic and copies ran while one was open for 1% -> 1% of each run, Pallas kernels for 5% -> 8%
where the time goes in v3:
time: 178 us; the launch traced here: 177 us
  starting transfers between devices  67.1 us (38%)
  waiting for transfers between devices  50.4 us (28%)
  Pallas kernels  30.7 us (17%)
  blocking collectives  25.4 us (14%)
    all_to_all x4, starting transfers between devices, swap(): return lax.all_to_all(x, axes, split_axis=0, concat_axis=0, tiled=True)  40.9 us
    all_to_all x4, waiting for transfers between devices, swap(): return lax.all_to_all(x, axes, split_axis=0, concat_axis=0, tiled=True)  38.3 us
    ppermute x9, starting transfers between devices, pass_on(): return lax.ppermute(x, 'section', ring)  26.2 us
    all_to_all x2, blocking collectives, swap(): return lax.all_to_all(x, axes, split_axis=0, concat_axis=0, tiled=True)  25.4 us
    ppermute x9, waiting for transfers between devices, pass_on(): return lax.ppermute(x, 'section', ring)  12.1 us
    pallas_call x1, Pallas kernels, row_grads(): pl.pallas_call(functools.partial(grad_kernel, list_len, part, scale, scal...  7.98 us
    pallas_call x1, Pallas kernels, row_attend(): pl.pallas_call(functools.partial(attend_kernel, list_len, part, scale2, r...  7.3 us
    pallas_call x1, Pallas kernels, row_stats(): pl.pallas_call(functools.partial(stats_kernel, list_len, part, scale2, ro...  4.95 us
  transfers between devices with their start and end apart: 13, of which 7 were waited for; matrix products, arithmetic and copies ran while one was open for 1% of the time, Pallas kernels for 8%

profile of v3, /device:TPU:1, one launch (start us, length us, event | category | flops | bytes accessed | tf_op | source)
XLA Modules:
  0.0 177.5 jit_solution(483189848819177849)
XLA Ops:
  2.2 16.7 %all-to-all-start = ((s32[32,1,1]{2,1,0:T(1,128)}), s32[32,1,1]{2,1,0:T(1,128)S(1)}, u32[]{:S(2)}, u32[]{:S(2)}) async-start(s32[32,1,1]{2,1,0:T(1,128)} %get-tuple-element.16), calls=%async_computation | async-start | bytes 32768 | tf_op jit(solution)/shard_map/all_to_all | solution.py:397
  20.1 10.6 %all-to-all-done.slot_ref = s32[32,1,1]{2,1,0:T(1,128)S(1)} async-done(((s32[32,1,1]{2,1,0:T(1,128)}), s32[32,1,1]{2,1,0:T(1,128)S(1)}, u32[]{:S(2)}, u32[]{:S(2)}) %all-to-all-start) | async-done | bytes 160 | tf_op jit(solution)/shard_map/all_to_all | solution.py:397
  32.4 4.6 %all-to-all-start.1 = ((bf16[32,64,128]{2,1,0:T(8,128)(2,1)}), bf16[32,64,128]{2,1,0:T(8,128)(2,1)S(1)}, u32[]{:S(2)}, u32[]{:S(2)}) async-start(bf16[32,64,128]{2,1,0:T(8,128)(2,1)} %pick.1), calls=%async_computation.1 | async-start | bytes 1048576 | tf_op jit(solution)/shard_map/all_to_all | solution.py:397
  37.0 3.1 %collective-permute-start = (bf16[2,1024,128]{2,1,0:T(8,128)(2,1)S(1)}, bf16[2,1024,128]{2,1,0:T(8,128)(2,1)S(1)}, u32[]{:S(2)}, u32[]{:S(2)}) collective-permute-start(bf16[2,1024,128]{2,1,0:T(8,128)(2,1)S(1)} %bitcast.24), channel_id=1, source_target_pairs={{0,128},{128,256},{256,384},{384,0},{1,129},{129,257},{257,385},{3... | collective-permute-start | bytes 1572872 | tf_op jit(solution)/shard_map/ppermute | solution.py:401
  40.1 3.4 %collective-permute-start.3 = (bf16[2,1024,128]{2,1,0:T(8,128)(2,1)S(1)}, bf16[2,1024,128]{2,1,0:T(8,128)(2,1)S(1)}, u32[]{:S(2)}, u32[]{:S(2)}) collective-permute-start(bf16[2,1024,128]{2,1,0:T(8,128)(2,1)S(1)} %bitcast.19), channel_id=1, source_target_pairs={{0,384},{128,0},{256,128},{384,256},{1,385},{129,1},{257,129},{385... | collective-permute-start | bytes 1572872 | tf_op jit(solution)/shard_map/ppermute | solution.py:401
  43.5 3.2 %collective-permute-start.1 = (bf16[2,1024,128]{2,1,0:T(8,128)(2,1)S(1)}, bf16[2,1024,128]{2,1,0:T(8,128)(2,1)S(1)}, u32[]{:S(2)}, u32[]{:S(2)}) collective-permute-start(bf16[2,1024,128]{2,1,0:T(8,128)(2,1)S(1)} %bitcast.25), channel_id=1, source_target_pairs={{0,384},{128,0},{256,128},{384,256},{1,385},{129,1},{257,129},{385... | collective-permute-start | bytes 1572872 | tf_op jit(solution)/shard_map/ppermute | solution.py:401
  46.7 2.1 %collective-permute-start.2 = (bf16[2,1024,128]{2,1,0:T(8,128)(2,1)S(1)}, bf16[2,1024,128]{2,1,0:T(8,128)(2,1)}, u32[]{:S(2)}, u32[]{:S(2)}) collective-permute-start(bf16[2,1024,128]{2,1,0:T(8,128)(2,1)S(1)} %bitcast.20), channel_id=1, source_target_pairs={{0,128},{128,256},{256,384},{384,0},{1,129},{129,257},{257,385},{3... | collective-permute-start | bytes 1572872 | tf_op jit(solution)/shard_map/ppermute | solution.py:401
  48.8 4.4 %collective-permute-done.refs_1_ = bf16[2,1024,128]{2,1,0:T(8,128)(2,1)S(1)} collective-permute-done((bf16[2,1024,128]{2,1,0:T(8,128)(2,1)S(1)}, bf16[2,1024,128]{2,1,0:T(8,128)(2,1)S(1)}, u32[]{:S(2)}, u32[]{:S(2)}) %collective-permute-start) | collective-permute-done | bytes 524320 | tf_op jit(solution)/shard_map/ppermute | solution.py:401
  55.1 4.6 %collective-permute-start.5 = (bf16[2,1024,128]{2,1,0:T(8,128)(2,1)S(1)}, bf16[2,1024,128]{2,1,0:T(8,128)(2,1)}, u32[]{:S(2)}, u32[]{:S(2)}) collective-permute-start(bf16[2,1024,128]{2,1,0:T(8,128)(2,1)S(1)} %collective-permute-done.3.refs_5_.refs_6_), channel_id=1, source_target_pairs={{0,384},{128,0},{256,128},{384,256},{1,385},{129,1},{257,129},{385... | collective-permute-start | bytes 1572872 | tf_op jit(solution)/shard_map/ppermute | solution.py:401
  59.7 6.5 %collective-permute-done.1.refs_2_ = bf16[2,1024,128]{2,1,0:T(8,128)(2,1)S(1)} collective-permute-done((bf16[2,1024,128]{2,1,0:T(8,128)(2,1)S(1)}, bf16[2,1024,128]{2,1,0:T(8,128)(2,1)S(1)}, u32[]{:S(2)}, u32[]{:S(2)}) %collective-permute-start.1) | collective-permute-done | bytes 524320 | tf_op jit(solution)/shard_map/ppermute | solution.py:401
  66.2 4.3 %all-to-all-done.1.arrived_ref = bf16[32,64,128]{2,1,0:T(8,128)(2,1)S(1)} async-done(((bf16[32,64,128]{2,1,0:T(8,128)(2,1)}), bf16[32,64,128]{2,1,0:T(8,128)(2,1)S(1)}, u32[]{:S(2)}, u32[]{:S(2)}) %all-to-all-start.1) | async-done | bytes 524320 | tf_op jit(solution)/shard_map/all_to_all | solution.py:397
  71.3 5.0 %stats.1.near_ref = f32[48,512]{1,0:T(8,128)} custom-call(s32[17]{0:T(128)} %get-tuple-element.15.table_ref, bf16[32,64,128]{2,1,0:T(8,128)(2,1)} %copy-done.5, bf16[2,1024,128]{2,1,0:T(8,128)(2,1)} %bitcast.21, bf16[2,1024,128]{2,1,0:T(8,128)(2,1)} %copy-done.9, bf16[2,1024,128]{2,1,0:T(8,128)(2,1)} %copy-done.10, bf16[2,1024,128]{2,1,0:T(8,128)(2,1)} %bitcast.17, ...), custom_call_target="tpu_custom_call" | custom-call | flops 805306368 | bytes 3145728 | tf_op jit(solution)/shard_map/stats/pallas_call | solution.py:249
  77.4 3.9 %far.1 = f32[4,48,512]{2,1,0:T(8,128)} custom-call(s32[17]{0:T(128)} %get-tuple-element.15.table_ref, bf16[32,64,128]{2,1,0:T(8,128)(2,1)} %copy-done.5, f32[48,512]{1,0:T(8,128)} %stats.1.near_ref, bf16[2,1024,128]{2,1,0:T(8,128)(2,1)} %collective-permute-done.4.q_hbm.refs_3_, bf16[2,1024,128]{2,1,0:T(8,128)(2,1)} %collective-permute-done.5.t_hbm.refs_7_), custom_call_target="tpu_custom_call" | custom-call | flops 268435456 | bytes 1048576 | tf_op jit(solution)/shard_map/far/pallas_call | solution.py:263
  81.4 10.4 %all_to_all.30.stats_ref = f32[4,48,512]{2,1,0:T(8,128)} all-to-all(f32[4,48,512]{2,1,0:T(8,128)} %far.1), channel_id=1, replica_groups=mesh['section'=4,'doc'=32,'mp'=4] {'section'}, dimensions={0} | all-to-all | bytes 786432 | tf_op jit(solution)/shard_map/all_to_all | solution.py:397
  91.8 8.0 %grads.1 = (bf16[32,64,128]{2,1,0:T(8,128)(2,1)}, f32[32,512]{1,0:T(8,128)}) custom-call(s32[17]{0:T(128)} %get-tuple-element.15.table_ref, bf16[32,64,128]{2,1,0:T(8,128)(2,1)} %copy-done.5, f32[4,48,512]{2,1,0:T(8,128)} %all_to_all.30.stats_ref, bf16[2,1024,128]{2,1,0:T(8,128)(2,1)} %bitcast.22, bf16[2,1024,128]{2,1,0:T(8,128)(2,1)} %copy-done.9, ...), custom_call_target="tpu_custom_call" | custom-call | flops 2147483648 | bytes 4194304 | tf_op jit(solution)/shard_map/grads/pallas_call | solution.py:281
  99.7 14.7 %all-to-all-start.3 = ((bf16[32,64,128]{2,1,0:T(8,128)(2,1)}), bf16[32,64,128]{2,1,0:T(8,128)(2,1)S(1)}, u32[]{:S(2)}, u32[]{:S(2)}) async-start(bf16[32,64,128]{2,1,0:T(8,128)(2,1)} %get-tuple-element.22), calls=%async_computation.3 | async-start | bytes 1048576 | tf_op jit(solution)/shard_map/all_to_all | solution.py:397
  114.5 7.3 %attend.1 = (bf16[2,1024,128]{2,1,0:T(8,128)(2,1)}, bf16[2,1024,128]{2,1,0:T(8,128)(2,1)}, bf16[2,1024,128]{2,1,0:T(8,128)(2,1)}, bf16[2,1024,128]{2,1,0:T(8,128)(2,1)}) custom-call(s32[17]{0:T(128)} %get-tuple-element.15.table_ref, bf16[32,64,128]{2,1,0:T(8,128)(2,1)} %copy-done.5, f32[32,512]{1,0:T(8,128)} %get-tuple-element.17.total_ref, ...), custom_call_target="tpu_custom_call" | custom-call | flops 1073741824 | bytes 4194304 | tf_op jit(solution)/shard_map/attend/pallas_call | solution.py:299
  121.8 2.9 %collective-permute-start.6 = (bf16[2,1024,128]{2,1,0:T(8,128)(2,1)}, bf16[2,1024,128]{2,1,0:T(8,128)(2,1)S(1)}, u32[]{:S(2)}, u32[]{:S(2)}) collective-permute-start(bf16[2,1024,128]{2,1,0:T(8,128)(2,1)} %get-tuple-element.19), channel_id=1, source_target_pairs={{0,384},{128,0},{256,128},{384,256},{1,385},{129,1},{257,129},{385... | collective-permute-start | bytes 1572872 | tf_op jit(solution)/shard_map/ppermute | solution.py:401
  124.7 2.5 %collective-permute-start.7 = (bf16[2,1024,128]{2,1,0:T(8,128)(2,1)}, bf16[2,1024,128]{2,1,0:T(8,128)(2,1)S(1)}, u32[]{:S(2)}, u32[]{:S(2)}) collective-permute-start(bf16[2,1024,128]{2,1,0:T(8,128)(2,1)} %get-tuple-element.20), channel_id=1, source_target_pairs={{0,128},{128,256},{256,384},{384,0},{1,129},{129,257},{257,385},{3... | collective-permute-start | bytes 1572872 | tf_op jit(solution)/shard_map/ppermute | solution.py:401
  127.2 2.5 %collective-permute-start.8 = (bf16[2,1024,128]{2,1,0:T(8,128)(2,1)}, bf16[2,1024,128]{2,1,0:T(8,128)(2,1)S(1)}, u32[]{:S(2)}, u32[]{:S(2)}) collective-permute-start(bf16[2,1024,128]{2,1,0:T(8,128)(2,1)} %get-tuple-element.21), channel_id=1, source_target_pairs={{0,256},{128,384},{256,0},{384,128},{1,257},{129,385},{257,1},{385... | collective-permute-start | bytes 1572872 | tf_op jit(solution)/shard_map/ppermute | solution.py:401
  129.7 18.2 %all-to-all-done.3.returned_ref = bf16[32,64,128]{2,1,0:T(8,128)(2,1)S(1)} async-done(((bf16[32,64,128]{2,1,0:T(8,128)(2,1)}), bf16[32,64,128]{2,1,0:T(8,128)(2,1)S(1)}, u32[]{:S(2)}, u32[]{:S(2)}) %all-to-all-start.3) | async-done | bytes 524320 | tf_op jit(solution)/shard_map/all_to_all | solution.py:397
  149.3 15.0 %all_to_all.31.square_ref = f32[32,1,128]{2,1,0:T(1,128)S(1)} all-to-all(f32[32,1,128]{2,1,0:T(1,128)S(1)} %get-tuple-element.23), channel_id=1, replica_groups=mesh['section'=4,'doc'=32,'mp'=4] {'doc'}, dimensions={0} | all-to-all | bytes 32768 | tf_op jit(solution)/shard_map/all_to_all | solution.py:397
  164.9 4.9 %all-to-all-start.5 = ((f32[16,1,128]{2,1,0:T(1,128)}), f32[16,1,128]{2,1,0:T(1,128)S(1)}, u32[]{:S(2)}, u32[]{:S(2)}) async-start(f32[16,1,128]{2,1,0:T(1,128)} %fold.1), calls=%async_computation.5 | async-start | bytes 16384 | tf_op jit(solution)/shard_map/all_to_all | solution.py:397
  171.0 5.2 %all-to-all-done.5.square_ref = f32[16,1,128]{2,1,0:T(1,128)S(1)} async-done(((f32[16,1,128]{2,1,0:T(1,128)}), f32[16,1,128]{2,1,0:T(1,128)S(1)}, u32[]{:S(2)}, u32[]{:S(2)}) %all-to-all-start.5) | async-done | bytes 8224 | tf_op jit(solution)/shard_map/all_to_all | solution.py:397
  (39 shorter events, 12.5 us)
Async XLA Ops:
  2.2 28.5 %all-to-all-start = ((s32[32,1,1]{2,1,0:T(1,128)}), s32[32,1,1]{2,1,0:T(1,128)S(1)}, u32[]{:S(2)}, u32[]{:S(2)}) async-start(s32[32,1,1]{2,1,0:T(1,128)} %get-tuple-element.16), calls=%async_computation | async-start | bytes 32768 | tf_op jit(solution)/shard_map/all_to_all | solution.py:397
  19.0 1.0 copy-start
  30.7 1.6 copy-start.3
  32.4 4.6 %copy-start.8 = (bf16[2,512,2,1,128]{4,2,3,1,0:T(2,128)(2,1)S(1)}, bf16[2,512,2,1,128]{4,2,3,1,0:T(2,128)(2,1)}, u32[]{:S(2)}) copy-start(bf16[2,512,2,1,128]{4,2,3,1,0:T(2,128)(2,1)} %param.6) | copy-start | bytes 1572868
  32.4 7.7 %copy-start.7 = (bf16[2,512,2,1,128]{4,2,3,1,0:T(2,128)(2,1)S(1)}, bf16[2,512,2,1,128]{4,2,3,1,0:T(2,128)(2,1)}, u32[]{:S(2)}) copy-start(bf16[2,512,2,1,128]{4,2,3,1,0:T(2,128)(2,1)} %param.7) | copy-start | bytes 1572868
  32.4 38.1 %all-to-all-start.1 = ((bf16[32,64,128]{2,1,0:T(8,128)(2,1)}), bf16[32,64,128]{2,1,0:T(8,128)(2,1)S(1)}, u32[]{:S(2)}, u32[]{:S(2)}) async-start(bf16[32,64,128]{2,1,0:T(8,128)(2,1)} %pick.1), calls=%async_computation.1 | async-start | bytes 1048576 | tf_op jit(solution)/shard_map/all_to_all | solution.py:397
  37.0 16.2 %collective-permute-start = (bf16[2,1024,128]{2,1,0:T(8,128)(2,1)S(1)}, bf16[2,1024,128]{2,1,0:T(8,128)(2,1)S(1)}, u32[]{:S(2)}, u32[]{:S(2)}) collective-permute-start(bf16[2,1024,128]{2,1,0:T(8,128)(2,1)S(1)} %bitcast.24), channel_id=1, source_target_pairs={{0,128},{128,256},{256,384},{384,0},{1,129},{129,257},{257,385},{3... | collective-permute-start | bytes 1572872 | tf_op jit(solution)/shard_map/ppermute | solution.py:401
  40.1 15.0 %collective-permute-start.3 = (bf16[2,1024,128]{2,1,0:T(8,128)(2,1)S(1)}, bf16[2,1024,128]{2,1,0:T(8,128)(2,1)S(1)}, u32[]{:S(2)}, u32[]{:S(2)}) collective-permute-start(bf16[2,1024,128]{2,1,0:T(8,128)(2,1)S(1)} %bitcast.19), channel_id=1, source_target_pairs={{0,384},{128,0},{256,128},{384,256},{1,385},{129,1},{257,129},{385... | collective-permute-start | bytes 1572872 | tf_op jit(solution)/shard_map/ppermute | solution.py:401
  43.5 22.7 %collective-permute-start.1 = (bf16[2,1024,128]{2,1,0:T(8,128)(2,1)S(1)}, bf16[2,1024,128]{2,1,0:T(8,128)(2,1)S(1)}, u32[]{:S(2)}, u32[]{:S(2)}) collective-permute-start(bf16[2,1024,128]{2,1,0:T(8,128)(2,1)S(1)} %bitcast.25), channel_id=1, source_target_pairs={{0,384},{128,0},{256,128},{384,256},{1,385},{129,1},{257,129},{385... | collective-permute-start | bytes 1572872 | tf_op jit(solution)/shard_map/ppermute | solution.py:401
  46.7 19.5 %collective-permute-start.2 = (bf16[2,1024,128]{2,1,0:T(8,128)(2,1)S(1)}, bf16[2,1024,128]{2,1,0:T(8,128)(2,1)}, u32[]{:S(2)}, u32[]{:S(2)}) collective-permute-start(bf16[2,1024,128]{2,1,0:T(8,128)(2,1)S(1)} %bitcast.20), channel_id=1, source_target_pairs={{0,128},{128,256},{256,384},{384,0},{1,129},{129,257},{257,385},{3... | collective-permute-start | bytes 1572872 | tf_op jit(solution)/shard_map/ppermute | solution.py:401
  53.2 17.3 %copy-start.9 = (bf16[2,1024,128]{2,1,0:T(8,128)(2,1)}, bf16[2,1024,128]{2,1,0:T(8,128)(2,1)S(1)}, u32[]{:S(2)}) copy-start(bf16[2,1024,128]{2,1,0:T(8,128)(2,1)S(1)} %collective-permute-done.refs_1_) | copy-start | bytes 1572868
  53.2 23.0 %collective-permute-start.4 = (bf16[2,1024,128]{2,1,0:T(8,128)(2,1)S(1)}, bf16[2,1024,128]{2,1,0:T(8,128)(2,1)}, u32[]{:S(2)}, u32[]{:S(2)}) collective-permute-start(bf16[2,1024,128]{2,1,0:T(8,128)(2,1)S(1)} %collective-permute-done.refs_1_), channel_id=1, source_target_pairs={{0,128},{128,256},{256,384},{384,0},{1,129},{129,257},{257,385},{3... | collective-permute-start | bytes 1572872 | tf_op jit(solution)/shard_map/ppermute | solution.py:401
  55.1 15.4 %copy-start.11 = (bf16[2,1024,128]{2,1,0:T(8,128)(2,1)}, bf16[2,1024,128]{2,1,0:T(8,128)(2,1)S(1)}, u32[]{:S(2)}) copy-start(bf16[2,1024,128]{2,1,0:T(8,128)(2,1)S(1)} %collective-permute-done.3.refs_5_.refs_6_) | copy-start | bytes 1572868
  55.1 22.3 %collective-permute-start.5 = (bf16[2,1024,128]{2,1,0:T(8,128)(2,1)S(1)}, bf16[2,1024,128]{2,1,0:T(8,128)(2,1)}, u32[]{:S(2)}, u32[]{:S(2)}) collective-permute-start(bf16[2,1024,128]{2,1,0:T(8,128)(2,1)S(1)} %collective-permute-done.3.refs_5_.refs_6_), channel_id=1, source_target_pairs={{0,384},{128,0},{256,128},{384,256},{1,385},{129,1},{257,129},{385... | collective-permute-start | bytes 1572872 | tf_op jit(solution)/shard_map/ppermute | solution.py:401
  66.2 4.3 %copy-start.10 = (bf16[2,1024,128]{2,1,0:T(8,128)(2,1)}, bf16[2,1024,128]{2,1,0:T(8,128)(2,1)S(1)}, u32[]{:S(2)}) copy-start(bf16[2,1024,128]{2,1,0:T(8,128)(2,1)S(1)} %collective-permute-done.1.refs_2_) | copy-start | bytes 1572868
  99.7 48.2 %all-to-all-start.3 = ((bf16[32,64,128]{2,1,0:T(8,128)(2,1)}), bf16[32,64,128]{2,1,0:T(8,128)(2,1)S(1)}, u32[]{:S(2)}, u32[]{:S(2)}) async-start(bf16[32,64,128]{2,1,0:T(8,128)(2,1)} %get-tuple-element.22), calls=%async_computation.3 | async-start | bytes 1048576 | tf_op jit(solution)/shard_map/all_to_all | solution.py:397
  114.4 33.5 %copy-start.4 = (s32[32,1,1]{2,1,0:T(1,128)S(1)}, s32[32,1,1]{2,1,0:T(1,128)}, u32[]{:S(2)}) copy-start(s32[32,1,1]{2,1,0:T(1,128)} %copy-done.3) | copy-start | bytes 388
  121.8 48.1 %copy-start.6 = (bf16[2,1024,128]{2,1,0:T(8,128)(2,1)S(1)}, bf16[2,1024,128]{2,1,0:T(8,128)(2,1)}, u32[]{:S(2)}) copy-start(bf16[2,1024,128]{2,1,0:T(8,128)(2,1)} %get-tuple-element.18) | copy-start | bytes 1572868
  121.8 48.1 %collective-permute-start.6 = (bf16[2,1024,128]{2,1,0:T(8,128)(2,1)}, bf16[2,1024,128]{2,1,0:T(8,128)(2,1)S(1)}, u32[]{:S(2)}, u32[]{:S(2)}) collective-permute-start(bf16[2,1024,128]{2,1,0:T(8,128)(2,1)} %get-tuple-element.19), channel_id=1, source_target_pairs={{0,384},{128,0},{256,128},{384,256},{1,385},{129,1},{257,129},{385... | collective-permute-start | bytes 1572872 | tf_op jit(solution)/shard_map/ppermute | solution.py:401
  124.7 45.1 %collective-permute-start.7 = (bf16[2,1024,128]{2,1,0:T(8,128)(2,1)}, bf16[2,1024,128]{2,1,0:T(8,128)(2,1)S(1)}, u32[]{:S(2)}, u32[]{:S(2)}) collective-permute-start(bf16[2,1024,128]{2,1,0:T(8,128)(2,1)} %get-tuple-element.20), channel_id=1, source_target_pairs={{0,128},{128,256},{256,384},{384,0},{1,129},{129,257},{257,385},{3... | collective-permute-start | bytes 1572872 | tf_op jit(solution)/shard_map/ppermute | solution.py:401
  127.2 42.7 %collective-permute-start.8 = (bf16[2,1024,128]{2,1,0:T(8,128)(2,1)}, bf16[2,1024,128]{2,1,0:T(8,128)(2,1)S(1)}, u32[]{:S(2)}, u32[]{:S(2)}) collective-permute-start(bf16[2,1024,128]{2,1,0:T(8,128)(2,1)} %get-tuple-element.21), channel_id=1, source_target_pairs={{0,256},{128,384},{256,0},{384,128},{1,257},{129,385},{257,1},{385... | collective-permute-start | bytes 1572872 | tf_op jit(solution)/shard_map/ppermute | solution.py:401
  164.9 11.3 %all-to-all-start.5 = ((f32[16,1,128]{2,1,0:T(1,128)}), f32[16,1,128]{2,1,0:T(1,128)S(1)}, u32[]{:S(2)}, u32[]{:S(2)}) async-start(f32[16,1,128]{2,1,0:T(1,128)} %fold.1), calls=%async_computation.5 | async-start | bytes 16384 | tf_op jit(solution)/shard_map/all_to_all | solution.py:397
  169.9 6.3 %copy-start.1 = (bf16[16,32,1,2,128]{4,3,2,1,0:T(2,128)(2,1)S(1)}, bf16[16,32,1,2,128]{4,3,2,1,0:T(2,128)(2,1)}, u32[]{:S(2)}) copy-start(bf16[16,32,1,2,128]{4,3,2,1,0:T(2,128)(2,1)} %param.8) | copy-start | bytes 786436
  169.9 6.3 %copy-start.2 = (f32[16,32,1,2,128]{4,3,2,1,0:T(2,128)S(1)}, f32[16,32,1,2,128]{4,3,2,1,0:T(2,128)}, u32[]{:S(2)}) copy-start(f32[16,32,1,2,128]{4,3,2,1,0:T(2,128)} %param.9) | copy-start | bytes 1572868
  (1 other events, 0.8 us)
